TPU v7x, 256 devices: a whole 4x4x8 slice. The times are simulated.
256 devices in a mesh: fold: 8 (over x, core), blk: 32 (over z, y).
Axes of the slice: x: 4, y: 4, z: 8, core: 2. Of those that a mesh axis runs over, the one named last changes fastest.
Arguments:
- fine_rhs: float32 [12288, 32, 128], P(('fold', 'blk')), may hold values from -6 to 6
- fine_tiles: bfloat16 [12288, 5, 128, 128], P(('fold', 'blk')), as said below
- fine_cols: int32 [12288, 5], P(('fold', 'blk')), may hold values from 0 to 12287, as said below
- fine_smoother: bfloat16 [12288, 128, 128], P(('fold', 'blk'))
- fine_map: int32 [12288], P(('fold', 'blk')), may hold values from 0 to 3071, as said below
- fine_slots: int32 [12288, 128], P(('fold', 'blk')), may hold values from 0 to 127
- mid_tiles: bfloat16 [3072, 5, 128, 128], P(('fold', 'blk'))
- mid_cols: int32 [3072, 5], P(('fold', 'blk')), may hold values from 0 to 3071, as said below
- mid_smoother: bfloat16 [3072, 128, 128], P(('fold', 'blk'))
- mid_map: int32 [3072], P(('fold', 'blk')), may hold values from 0 to 767, as said below
- mid_slots: int32 [3072, 128], P(('fold', 'blk')), may hold values from 0 to 127
- coarse_tiles: bfloat16 [768, 5, 128, 128], P('blk')
- coarse_cols: int32 [768, 5], P('blk'), may hold values from 0 to 767, as said below
- coarse_smoother: bfloat16 [768, 128, 128], P('blk')
Outputs:
- fine_field: float32 [12288, 32, 128], P(('fold', 'blk'))
- mid_field: float32 [3072, 32, 128], P(('fold', 'blk'))
- coarse_field: float32 [768, 32, 128], P('blk')
Inputs may be any that keep to these rules, and one draw needn't show every extreme that they name: `fine_cols`: column 0 of each row names the row's own block; every other entry names a level-0 block of a device with the same fold index whose blk index differs by at most one, cyclically. `mid_cols`: column 0 of each row names the row's own block; every other entry names a level-1 block of a device with the same fold index whose blk index differs by at most one, cyclically. `coarse_cols`: column 0 of each row names the row's own block; every other entry names a level-2 block whose blk index differs from the row's by at most one, cyclically. `fine_map`: A level-0 block's level-1 block lies on a device with the same fold index; of the level-0 blocks of one device at most 3 have their level-1 blocks on any one device, and in every fold row some device receives exactly 3 from every device of that row. `mid_map`: A level-1 block's level-2 block lies at the same blk index. `fine_tiles`: each smoother tile is close to half the inverse of the diagonal of the row block's diagonal tile.
All inputs are finite; a program needn't handle non-finite values.
Results may differ from a plain program's by a relative error of at most 0.012.
Values may be sent and summed in bfloat16 or wider, within the bound.
A program may use at most 128 MiB of HBM per device.

v0:
```python
import jax
import jax.numpy as jnp
from jax import lax
from jax.sharding import PartitionSpec as P

VB = 128
COARSE = 8


def extended(value, sides, width):
    for axis, dim in sides:
        size, length = (lax.axis_size(axis), value.shape[dim])
        up = [(i, (i + 1) % size) for i in range(size)]
        down = [(j, i) for i, j in up]
        last = lax.slice_in_dim(value, length - width, length, axis=dim)
        first = lax.slice_in_dim(value, 0, width, axis=dim)
        before = lax.ppermute(last, axis, up)
        after = lax.ppermute(first, axis, down)
        value = jnp.concatenate([before, value, after], axis=dim)
    return value


def apply_tiles(tiles, columns, rough):
    per_device = rough.shape[0]
    blk_count = lax.axis_size("blk")
    widened = extended(rough, (("blk", 0),), per_device)
    my_blk = lax.axis_index("blk")
    owner = columns // per_device % blk_count
    offset = (owner - my_blk + 1 + blk_count) % blk_count
    local_index = offset * per_device + columns % per_device
    chooser = (
        local_index[:, :, None] == jnp.arange(widened.shape[0], dtype=jnp.int32)[None, None, :]
    ).astype(jnp.bfloat16)
    picked = jnp.einsum(
        "ikj,jrw->ikrw", chooser, widened, preferred_element_type=jnp.float32
    ).astype(jnp.bfloat16)
    return jnp.einsum("ikuw,ikrw->iru", tiles, picked, preferred_element_type=jnp.float32)


def smooth_tiles(smoother, resid):
    return jnp.einsum(
        "iuw,irw->iru", smoother, resid.astype(jnp.bfloat16), preferred_element_type=jnp.float32
    )


def sweep_level(tiles, columns, smoother, rhs_field, field):
    return field + smooth_tiles(
        smoother, rhs_field - apply_tiles(tiles, columns, field.astype(jnp.bfloat16))
    )


def slot_table(slots):
    return (slots[:, :, None] == jnp.arange(VB, dtype=jnp.int32)[None, None, :]).astype(jnp.float32)


def collect_slots(field, table):
    return jnp.einsum("jrv,jvs->jrs", field, table, precision=lax.Precision.HIGHEST)


def spread_slots(coarse, table):
    return jnp.einsum("jrs,jvs->jrv", coarse, table, precision=lax.Precision.HIGHEST)


def on_device(
    fine_rhs,
    fine_tiles,
    fine_cols,
    fine_smoother,
    fine_map,
    fine_slots,
    mid_tiles,
    mid_cols,
    mid_smoother,
    mid_map,
    mid_slots,
    coarse_tiles,
    coarse_cols,
    coarse_smoother,
):
    mid_count = mid_tiles.shape[0]
    low_count = coarse_tiles.shape[0]
    blk_count = lax.axis_size("blk")
    fine_table = slot_table(fine_slots)
    mid_table = slot_table(mid_slots)
    fine_pre = smooth_tiles(fine_smoother, fine_rhs)
    fine_pre = sweep_level(fine_tiles, fine_cols, fine_smoother, fine_rhs, fine_pre)
    fine_resid = fine_rhs - apply_tiles(fine_tiles, fine_cols, fine_pre.astype(jnp.bfloat16))
    pieces = collect_slots(fine_resid, fine_table)
    destination = fine_map // mid_count % blk_count
    target = fine_map % mid_count
    flat_index = destination * mid_count + target
    wanted = jnp.arange(mid_count * lax.axis_size("blk"), dtype=jnp.int32)
    picking = (wanted[:, None] == flat_index[None, :]).astype(jnp.float32)
    mid_rhs = lax.psum_scatter(
        jnp.einsum("tj,jrs->trs", picking, pieces, precision=lax.Precision.HIGHEST),
        "blk",
        scatter_dimension=0,
        tiled=True,
    )
    mid_pre = smooth_tiles(mid_smoother, mid_rhs)
    mid_pre = sweep_level(mid_tiles, mid_cols, mid_smoother, mid_rhs, mid_pre)
    mid_resid = mid_rhs - apply_tiles(mid_tiles, mid_cols, mid_pre.astype(jnp.bfloat16))
    low_index = mid_map % low_count
    low_pick = (jnp.arange(low_count, dtype=jnp.int32)[:, None] == low_index[None, :]).astype(
        jnp.float32
    )
    low_terms = jnp.einsum(
        "tj,jrs->trs",
        low_pick,
        collect_slots(mid_resid, mid_table),
        precision=lax.Precision.HIGHEST,
    )
    coarse_rhs = lax.psum(low_terms.astype(jnp.bfloat16), "fold").astype(jnp.float32)
    coarse_field = smooth_tiles(coarse_smoother, coarse_rhs)

    def full_sweep(sweep_turn, field):
        return sweep_level(coarse_tiles, coarse_cols, coarse_smoother, coarse_rhs, field)

    coarse_field = lax.fori_loop(0, COARSE - 1, full_sweep, coarse_field)
    lifted = jnp.einsum("tj,trs->jrs", low_pick, coarse_field, precision=lax.Precision.HIGHEST)
    mid_field = mid_pre + spread_slots(lifted, mid_table)
    mid_field = sweep_level(mid_tiles, mid_cols, mid_smoother, mid_rhs, mid_field)
    whole_mid = lax.all_gather(mid_field.astype(jnp.bfloat16), "blk", axis=0, tiled=True).astype(
        mid_field.dtype
    )
    choose_rows = (
        flat_index[:, None] == jnp.arange(whole_mid.shape[0], dtype=jnp.int32)[None, :]
    ).astype(jnp.float32)
    fine_coarse = jnp.einsum("jq,qrs->jrs", choose_rows, whole_mid, precision=lax.Precision.HIGHEST)
    fine_field = fine_pre + spread_slots(fine_coarse, fine_table)
    fine_field = sweep_level(fine_tiles, fine_cols, fine_smoother, fine_rhs, fine_field)
    return (fine_field, mid_field, coarse_field)


def solution(mesh):
    placed = (
        P(("fold", "blk"), None, None),
        P(("fold", "blk"), None, None, None),
        P(("fold", "blk"), None),
        P(("fold", "blk"), None, None),
        P(("fold", "blk")),
        P(("fold", "blk"), None),
        P(("fold", "blk"), None, None, None),
        P(("fold", "blk"), None),
        P(("fold", "blk"), None, None),
        P(("fold", "blk")),
        P(("fold", "blk"), None),
        P("blk", None, None, None),
        P("blk", None),
        P("blk", None, None),
    )
    return jax.shard_map(
        on_device,
        mesh=mesh,
        in_specs=placed,
        out_specs=(
            P(("fold", "blk"), None, None),
            P(("fold", "blk"), None, None),
            P("blk", None, None),
        ),
        check_vma=False,
    )
```

profile of v0, /device:TPU:1, one launch (start us, length us, event | category | flops | bytes accessed | tf_op | source)
XLA Modules:
  0.0 616.6 jit_solution(433488977866551041)
XLA Ops:
  10.8 8.9 %collective-permute-start.3 = (bf16[48,32,128]{2,1,0:T(8,128)(2,1)S(1)}, bf16[48,32,128]{2,1,0:T(8,128)(2,1)S(1)}, u32[]{:S(2)}, u32[]{:S(2)}) collective-permute-start(bf16[48,32,128]{2,1,0:T(8,128)(2,1)S(1)} %get-tuple-element.150), channel_id=1, source_target_pairs={{1,0},{2,1},{3,2},{4,3},{5,4},{6,5},{7,6},{8,7},{9,8},{10,9},{11,1... | collective-permute-start | bytes 1179656 | tf_op jit(solution)/shard_map/ppermute | solution.py:18
  20.0 7.5 %collective-permute-done.3 = bf16[48,32,128]{2,1,0:T(8,128)(2,1)S(1)} collective-permute-done((bf16[48,32,128]{2,1,0:T(8,128)(2,1)S(1)}, bf16[48,32,128]{2,1,0:T(8,128)(2,1)S(1)}, u32[]{:S(2)}, u32[]{:S(2)}) %collective-permute-start.3) | collective-permute-done | bytes 393248 | tf_op jit(solution)/shard_map/ppermute | solution.py:18
  27.5 5.2 collective-permute-done.2
  34.9 8.8 %fusion.100 = (bf16[48,32,128]{2,1,0:T(8,128)(2,1)}, f32[48,32,128]{2,1,0:T(8,128)}) fusion(f32[48,32,128]{2,1,0:T(8,128)} %get-tuple-element.151, bf16[48,128,128]{2,1,0:T(8,128)(2,1)S(1)} %copy-done.2, f32[48,32,128]{2,1,0:T(8,128)} %param.16, bf16[48,5,128,128]{3,2,1,0:T(8,128)(2,1)} %param.17, bf16[48,5,32,128]{3,0,2,1:T(8,128)(2,1)} %fusion.34), kind=kOutput, calls=%fused_computation.163 | convolution fusion | flops 302776320 | bytes 14155776 | tf_op jit(solution)/shard_map/iuw,irw->iru/dot_general | solution.py:41
  45.2 7.5 %collective-permute-done.5 = bf16[48,32,128]{2,1,0:T(8,128)(2,1)S(1)} collective-permute-done((bf16[48,32,128]{2,1,0:T(8,128)(2,1)}, bf16[48,32,128]{2,1,0:T(8,128)(2,1)S(1)}, u32[]{:S(2)}, u32[]{:S(2)}) %collective-permute-start.5) | collective-permute-done | bytes 393248 | tf_op jit(solution)/shard_map/ppermute | solution.py:18
  58.6 5.0 fusion.25
  69.3 6.3 %copy.27 = f32[384,32,128]{2,1,0:T(8,128)} copy(f32[384,32,128]{2,0,1:T(8,128)S(1)} %fusion.42) | data formatting | bytes 12582912 | tf_op jit(solution)/shard_map/tj,jrs->trs/dot_general | solution.py:95
  76.4 216.9 %reduce-scatter.2.cloned.1.call-done = f32[12,32,128]{2,1,0:T(8,128)} async-done(((f32[384,32,128]{2,1,0:T(8,128)}), f32[12,32,128]{2,1,0:T(8,128)}) %reduce-scatter.2.cloned.1.call-update) | async-done | bytes 196624 | tf_op jit(solution)/shard_map/reduce_scatter | solution.py:94
  299.4 5.1 collective-permute-done.6
  318.0 66.1 %all-reduce.2.cloned.1.call-done = bf16[24,32,128]{2,0,1:T(8,128)(2,1)} async-done(((bf16[24,32,128]{2,0,1:T(8,128)(2,1)}), bf16[24,32,128]{2,0,1:T(8,128)(2,1)}) %all-reduce.2.cloned.1.call-update) | async-done | bytes 196624 | tf_op jit(solution)/shard_map/psum | solution.py:113
  387.5 95.2 %while.13 = (s32[]{:T(128)}, f32[24,32,128]{2,1,0:T(8,128)S(1)}, s32[24,5,1]{0,1,2:T(8,128)}, s32[24,5]{0,1:T(8,128)S(1)}, bf16[24,5,128,128]{3,2,1,0:T(8,128)(2...) while((s32[]{:T(128)}, f32[24,32,128]{2,1,0:T(8,128)S(1)}, ...), condition=%wide.region_3.4_spmd, body=%wide.region_2.3_spmd.sunk | while | flops 222769952 | bytes 11816837 | solution.py:119
  387.6 5.3 collective-permute-start
  395.5 5.2 collective-permute-done.1
  401.2 4.3 convolution_add_fusion.7
  414.1 4.3 convolution_add_fusion.7
  427.0 4.3 convolution_add_fusion.7
  439.8 4.3 convolution_add_fusion.7
  452.7 4.3 convolution_add_fusion.7
  465.6 4.3 convolution_add_fusion.7
  478.4 4.3 convolution_add_fusion.7
  496.7 83.8 %all-gather.2.cloned.1.call-done = bf16[384,32,128]{2,1,0:T(8,128)(2,1)} async-done(((bf16[12,32,128]{2,1,0:T(8,128)(2,1)}), bf16[384,32,128]{2,1,0:T(8,128)(2,1)}) %all-gather.2.cloned.1.call-update) | async-done | bytes 3145744 | tf_op jit(solution)/shard_map/all_gather | solution.py:123
  589.2 4.9 collective-permute-done.13
  594.1 5.1 collective-permute-done.12
  601.4 8.7 %convolution_add_fusion.1 = f32[48,32,128]{2,1,0:T(8,128)} fusion(f32[48,32,128]{2,1,0:T(8,128)} %get-tuple-element.163, bf16[48,128,128]{2,1,0:T(8,128)(2,1)S(1)} %copy-done.3, f32[48,32,128]{2,1,0:T(8,128)} %param.16, bf16[48,5,128,128]{3,2,1,0:T(8,128)(2,1)} %param.17, bf16[48,5,32,128]{3,0,2,1:T(8,128)(2,1)} %fusion.30), kind=kOutput, calls=%fused_computation.40 | convolution fusion | flops 302579712 | bytes 13762560 | tf_op jit(solution)/shard_map/iuw,irw->iru/dot_general | solution.py:41
  (173 shorter events, 121.8 us)
Async XLA Ops:
  7.2 286.1 %reduce-scatter.2.cloned.1.call-start = ((), (), s32[]{:S(2)}) async-start(), calls=%async_computation.1 | async-start | bytes 6488064 | tf_op jit(solution)/shard_map/reduce_scatter | solution.py:94
  10.8 16.6 %collective-permute-start.3 = (bf16[48,32,128]{2,1,0:T(8,128)(2,1)S(1)}, bf16[48,32,128]{2,1,0:T(8,128)(2,1)S(1)}, u32[]{:S(2)}, u32[]{:S(2)}) collective-permute-start(bf16[48,32,128]{2,1,0:T(8,128)(2,1)S(1)} %get-tuple-element.150), channel_id=1, source_target_pairs={{1,0},{2,1},{3,2},{4,3},{5,4},{6,5},{7,6},{8,7},{9,8},{10,9},{11,1... | collective-permute-start | bytes 1179656 | tf_op jit(solution)/shard_map/ppermute | solution.py:18
  19.7 13.0 %collective-permute-start.2 = (bf16[48,32,128]{2,1,0:T(8,128)(2,1)S(1)}, bf16[48,32,128]{2,1,0:T(8,128)(2,1)S(1)}, u32[]{:S(2)}, u32[]{:S(2)}) collective-permute-start(bf16[48,32,128]{2,1,0:T(8,128)(2,1)S(1)} %get-tuple-element.150), channel_id=1, source_target_pairs={{0,1},{1,2},{2,3},{3,4},{4,5},{5,6},{6,7},{7,8},{8,9},{9,10},{10,1... | collective-permute-start | bytes 1179656 | tf_op jit(solution)/shard_map/ppermute | solution.py:17
  43.7 9.0 %collective-permute-start.5 = (bf16[48,32,128]{2,1,0:T(8,128)(2,1)}, bf16[48,32,128]{2,1,0:T(8,128)(2,1)S(1)}, u32[]{:S(2)}, u32[]{:S(2)}) collective-permute-start(bf16[48,32,128]{2,1,0:T(8,128)(2,1)} %get-tuple-element.152), channel_id=1, source_target_pairs={{1,0},{2,1},{3,2},{4,3},{5,4},{6,5},{7,6},{8,7},{9,8},{10,9},{11,1... | collective-permute-start | bytes 1179656 | tf_op jit(solution)/shard_map/ppermute | solution.py:18
  44.0 12.3 %collective-permute-start.4 = (bf16[48,32,128]{2,1,0:T(8,128)(2,1)}, bf16[48,32,128]{2,1,0:T(8,128)(2,1)S(1)}, u32[]{:S(2)}, u32[]{:S(2)}) collective-permute-start(bf16[48,32,128]{2,1,0:T(8,128)(2,1)} %get-tuple-element.152), channel_id=1, source_target_pairs={{0,1},{1,2},{2,3},{3,4},{4,5},{5,6},{6,7},{7,8},{8,9},{9,10},{10,1... | collective-permute-start | bytes 1179656 | tf_op jit(solution)/shard_map/ppermute | solution.py:17
  75.6 308.5 %all-reduce.2.cloned.1.call-start = ((), (), s32[]{:S(2)}) async-start(), calls=%async_computation.2 | async-start | bytes 393216 | tf_op jit(solution)/shard_map/psum | solution.py:113
  297.8 6.8 %collective-permute-start.6 = (bf16[12,32,128]{2,1,0:T(8,128)(2,1)S(1)}, bf16[12,32,128]{2,1,0:T(8,128)(2,1)S(1)}, u32[]{:S(2)}, u32[]{:S(2)}) collective-permute-start(bf16[12,32,128]{2,1,0:T(8,128)(2,1)S(1)} %get-tuple-element.154), channel_id=1, source_target_pairs={{0,1},{1,2},{2,3},{3,4},{4,5},{5,6},{6,7},{7,8},{8,9},{9,10},{10,1... | collective-permute-start | bytes 294920 | tf_op jit(solution)/shard_map/ppermute | solution.py:17
  307.6 6.8 %collective-permute-start.8 = (bf16[12,32,128]{2,1,0:T(8,128)(2,1)S(1)}, bf16[12,32,128]{2,1,0:T(8,128)(2,1)S(1)}, u32[]{:S(2)}, u32[]{:S(2)}) collective-permute-start(bf16[12,32,128]{2,1,0:T(8,128)(2,1)S(1)} %get-tuple-element.156), channel_id=1, source_target_pairs={{0,1},{1,2},{2,3},{3,4},{4,5},{5,6},{6,7},{7,8},{8,9},{9,10},{10,1... | collective-permute-start | bytes 294920 | tf_op jit(solution)/shard_map/ppermute | solution.py:17
  317.3 263.2 %all-gather.2.cloned.1.call-start = ((), (), s32[]{:S(2)}) async-start(), calls=%async_computation.3 | async-start | bytes 3244032 | tf_op jit(solution)/shard_map/all_gather | solution.py:123
  387.6 7.9 %collective-permute-start = (bf16[24,32,128]{2,1,0:T(8,128)(2,1)S(1)}, bf16[24,32,128]{2,1,0:T(8,128)(2,1)S(1)}, u32[]{:S(2)}, u32[]{:S(2)}) collective-permute-start(bf16[24,32,128]{2,1,0:T(8,128)(2,1)S(1)} %convert_element_type.196), channel_id=1, source_target_pairs={{1,0},{2,1},{3,2},{4,3},{5,4},{6,5},{7,6},{8,7},{9,8},{10,9},{11,1... | collective-permute-start | bytes 589832 | tf_op jit(solution)/shard_map/while/body/eval_jaxpr/ppermute | solution.py:18
  392.9 7.8 %collective-permute-start.1 = (bf16[24,32,128]{2,1,0:T(8,128)(2,1)S(1)}, bf16[24,32,128]{2,1,0:T(8,128)(2,1)S(1)}, u32[]{:S(2)}, u32[]{:S(2)}) collective-permute-start(bf16[24,32,128]{2,1,0:T(8,128)(2,1)S(1)} %convert_element_type.196), channel_id=1, source_target_pairs={{0,1},{1,2},{2,3},{3,4},{4,5},{5,6},{6,7},{7,8},{8,9},{9,10},{10,1... | collective-permute-start | bytes 589832 | tf_op jit(solution)/shard_map/while/body/eval_jaxpr/ppermute | solution.py:17
  405.6 4.6 collective-permute-start
  405.7 7.9 %collective-permute-start.1 = (bf16[24,32,128]{2,1,0:T(8,128)(2,1)S(1)}, bf16[24,32,128]{2,1,0:T(8,128)(2,1)S(1)}, u32[]{:S(2)}, u32[]{:S(2)}) collective-permute-start(bf16[24,32,128]{2,1,0:T(8,128)(2,1)S(1)} %convert_element_type.196), channel_id=1, source_target_pairs={{0,1},{1,2},{2,3},{3,4},{4,5},{5,6},{6,7},{7,8},{8,9},{9,10},{10,1... | collective-permute-start | bytes 589832 | tf_op jit(solution)/shard_map/while/body/eval_jaxpr/ppermute | solution.py:17
  418.5 4.6 collective-permute-start
  418.5 7.9 %collective-permute-start.1 = (bf16[24,32,128]{2,1,0:T(8,128)(2,1)S(1)}, bf16[24,32,128]{2,1,0:T(8,128)(2,1)S(1)}, u32[]{:S(2)}, u32[]{:S(2)}) collective-permute-start(bf16[24,32,128]{2,1,0:T(8,128)(2,1)S(1)} %convert_element_type.196), channel_id=1, source_target_pairs={{0,1},{1,2},{2,3},{3,4},{4,5},{5,6},{6,7},{7,8},{8,9},{9,10},{10,1... | collective-permute-start | bytes 589832 | tf_op jit(solution)/shard_map/while/body/eval_jaxpr/ppermute | solution.py:17
  431.3 4.6 collective-permute-start
  431.4 7.9 %collective-permute-start.1 = (bf16[24,32,128]{2,1,0:T(8,128)(2,1)S(1)}, bf16[24,32,128]{2,1,0:T(8,128)(2,1)S(1)}, u32[]{:S(2)}, u32[]{:S(2)}) collective-permute-start(bf16[24,32,128]{2,1,0:T(8,128)(2,1)S(1)} %convert_element_type.196), channel_id=1, source_target_pairs={{0,1},{1,2},{2,3},{3,4},{4,5},{5,6},{6,7},{7,8},{8,9},{9,10},{10,1... | collective-permute-start | bytes 589832 | tf_op jit(solution)/shard_map/while/body/eval_jaxpr/ppermute | solution.py:17
  444.3 7.9 %collective-permute-start.1 = (bf16[24,32,128]{2,1,0:T(8,128)(2,1)S(1)}, bf16[24,32,128]{2,1,0:T(8,128)(2,1)S(1)}, u32[]{:S(2)}, u32[]{:S(2)}) collective-permute-start(bf16[24,32,128]{2,1,0:T(8,128)(2,1)S(1)} %convert_element_type.196), channel_id=1, source_target_pairs={{0,1},{1,2},{2,3},{3,4},{4,5},{5,6},{6,7},{7,8},{8,9},{9,10},{10,1... | collective-permute-start | bytes 589832 | tf_op jit(solution)/shard_map/while/body/eval_jaxpr/ppermute | solution.py:17
  457.2 7.9 %collective-permute-start.1 = (bf16[24,32,128]{2,1,0:T(8,128)(2,1)S(1)}, bf16[24,32,128]{2,1,0:T(8,128)(2,1)S(1)}, u32[]{:S(2)}, u32[]{:S(2)}) collective-permute-start(bf16[24,32,128]{2,1,0:T(8,128)(2,1)S(1)} %convert_element_type.196), channel_id=1, source_target_pairs={{0,1},{1,2},{2,3},{3,4},{4,5},{5,6},{6,7},{7,8},{8,9},{9,10},{10,1... | collective-permute-start | bytes 589832 | tf_op jit(solution)/shard_map/while/body/eval_jaxpr/ppermute | solution.py:17
  469.9 4.7 collective-permute-start
  470.0 7.9 %collective-permute-start.1 = (bf16[24,32,128]{2,1,0:T(8,128)(2,1)S(1)}, bf16[24,32,128]{2,1,0:T(8,128)(2,1)S(1)}, u32[]{:S(2)}, u32[]{:S(2)}) collective-permute-start(bf16[24,32,128]{2,1,0:T(8,128)(2,1)S(1)} %convert_element_type.196), channel_id=1, source_target_pairs={{0,1},{1,2},{2,3},{3,4},{4,5},{5,6},{6,7},{7,8},{8,9},{9,10},{10,1... | collective-permute-start | bytes 589832 | tf_op jit(solution)/shard_map/while/body/eval_jaxpr/ppermute | solution.py:17
  485.8 6.9 %collective-permute-start.10 = (bf16[12,32,128]{2,1,0:T(8,128)(2,1)S(1)}, bf16[12,32,128]{2,1,0:T(8,128)(2,1)S(1)}, u32[]{:S(2)}, u32[]{:S(2)}) collective-permute-start(bf16[12,32,128]{2,1,0:T(8,128)(2,1)S(1)} %get-tuple-element.158), channel_id=1, source_target_pairs={{0,1},{1,2},{2,3},{3,4},{4,5},{5,6},{6,7},{7,8},{8,9},{9,10},{10,1... | collective-permute-start | bytes 294920 | tf_op jit(solution)/shard_map/ppermute | solution.py:17
  587.5 6.6 %collective-permute-start.13 = (bf16[48,32,128]{2,1,0:T(8,128)(2,1)S(1)}, bf16[48,32,128]{2,1,0:T(8,128)(2,1)S(1)}, u32[]{:S(2)}, u32[]{:S(2)}) collective-permute-start(bf16[48,32,128]{2,1,0:T(8,128)(2,1)S(1)} %get-tuple-element.162), channel_id=1, source_target_pairs={{1,0},{2,1},{3,2},{4,3},{5,4},{6,5},{7,6},{8,7},{9,8},{10,9},{11,1... | collective-permute-start | bytes 1179656 | tf_op jit(solution)/shard_map/ppermute | solution.py:18
  589.2 9.9 %collective-permute-start.12 = (bf16[48,32,128]{2,1,0:T(8,128)(2,1)S(1)}, bf16[48,32,128]{2,1,0:T(8,128)(2,1)S(1)}, u32[]{:S(2)}, u32[]{:S(2)}) collective-permute-start(bf16[48,32,128]{2,1,0:T(8,128)(2,1)S(1)} %get-tuple-element.162), channel_id=1, source_target_pairs={{0,1},{1,2},{2,3},{3,4},{4,5},{5,6},{6,7},{7,8},{8,9},{9,10},{10,1... | collective-permute-start | bytes 1179656 | tf_op jit(solution)/shard_map/ppermute | solution.py:17
  (28 other events, 947.3 us)
Sparse Core Ops, SparseCore 0:
  75.7 217.5 reduce-scatter.1
  317.4 66.6 all-reduce.1
  496.8 83.6 all-gather.1
where the time goes:
time: 622 us; the launch traced here: 617 us
  waiting for transfers between devices  458 us (74%)
  matrix products  93 us (15%)
  starting transfers between devices  32.1 us (5%)
  between operations  14.1 us (2%)
  local copies, waits for them, and re-layouts  9.95 us (2%)
  other arithmetic  8.65 us (1%)
    reduce_scatter x1, waiting for transfers between devices, on_device(): lax.psum_scatter(jnp.einsum('tj,jrs->trs', picking, pieces, precision=lax...  217 us
    all_gather x1, waiting for transfers between devices, on_device(): lax.all_gather(mid_field.astype(jnp.bfloat16), 'blk', axis=0, tiled=True)  83.8 us
    psum x1, waiting for transfers between devices, on_device(): lax.psum(low_terms.astype(jnp.bfloat16), 'fold').astype(jnp.float32)  66.1 us
    dot_general x14, matrix products, smooth_tiles(): jnp.einsum('iuw,irw->iru', smoother, resid.astype(jnp.bfloat16), preferre...  60.3 us
    ppermute x13, waiting for transfers between devices, extended(): before = lax.ppermute(last, axis, up)  51.4 us
    ppermute x13, waiting for transfers between devices, extended(): after = lax.ppermute(first, axis, down)  40.2 us
    ppermute x13, starting transfers between devices, extended(): after = lax.ppermute(first, axis, down)  19.2 us
    ppermute x13, starting transfers between devices, extended(): before = lax.ppermute(last, axis, up)  12.8 us
  transfers between devices with their start and end apart: 29, of which 29 were waited for; matrix products, arithmetic and copies ran while one was open for 1% of the time, Pallas kernels for 0%

commit v1 on v0

v1 whole, which is shorter than its diff:
```python
import functools

import jax
import jax.numpy as jnp
from jax import lax
from jax.experimental import pallas as pl
from jax.experimental.pallas import tpu as pltpu
from jax.sharding import PartitionSpec as P

COARSE = 8
CAP = 3
CHUNKS = 4
MESH = pl.DeviceIdType.MESH
F32 = jnp.float32
BF16 = jnp.bfloat16


def times(left, right):
    return lax.dot_general(
        left, right, (((1,), (1,)), ((), ())), preferred_element_type=F32
    )


def group_of(count, most):
    return max(size for size in range(1, most + 1) if count % size == 0)


def for_rows(start, count, body, most=4):
    size = group_of(count, most)

    def step(turn, carry):
        first = start + turn * size
        body([first + k for k in range(size)])
        return carry

    lax.fori_loop(0, count // size, step, 0)


def applied(tiles, cols, wide, row, stored):
    picked = jnp.concatenate(
        [wide[cols[row * stored + k]] for k in range(stored)], axis=1
    )
    tile = jnp.concatenate([tiles[row, k] for k in range(stored)], axis=1)
    return times(picked, tile)


def chosen(slots, row):
    line = slots[pl.ds(row, 1), :]
    width = line.shape[1]
    places = lax.broadcasted_iota(jnp.int32, (width, width), 0)
    return jnp.where(places == line, 1.0, 0.0).astype(BF16)


class Links:
    def __init__(self):
        self.fold = lax.axis_index("fold")
        self.blk = lax.axis_index("blk")
        self.folds = lax.axis_size("fold")
        self.blks = lax.axis_size("blk")

    def along_blk(self, step):
        return (self.fold, lax.rem(self.blk + step + self.blks, self.blks))

    def along_fold(self, step):
        return (lax.rem(self.fold + step, self.folds), self.blk)

    def greet_blk(self, barrier):
        def step(k, carry):
            pl.semaphore_signal(
                barrier, inc=1, device_id=self.along_blk(k), device_id_type=MESH
            )
            return carry

        lax.fori_loop(1, self.blks, step, 0)

    def greet_fold(self, barrier):
        def step(k, carry):
            pl.semaphore_signal(
                barrier, inc=1, device_id=self.along_fold(k), device_id_type=MESH
            )
            return carry

        lax.fori_loop(1, self.folds, step, 0)


def remote(source, target, send, recv, device):
    return pltpu.make_async_remote_copy(
        src_ref=source,
        dst_ref=target,
        send_sem=send,
        recv_sem=recv,
        device_id=device,
        device_id_type=MESH,
    )


def halo_copies(links, wide, count, first, rows, send, recv, part):
    own = wide.at[pl.ds(count + first, rows)]
    up = remote(
        own,
        wide.at[pl.ds(first, rows)],
        send.at[0, part],
        recv.at[0, part],
        links.along_blk(1),
    )
    down = remote(
        own,
        wide.at[pl.ds(2 * count + first, rows)],
        send.at[1, part],
        recv.at[1, part],
        links.along_blk(-1),
    )
    return up, down


def down_kernel(
    cols,
    sidx,
    rhs_h,
    tiles_h,
    smo_h,
    slots,
    goals,
    pre_o,
    recv_o,
    goals_o,
    rhs,
    tiles,
    smo,
    pre,
    wide0,
    wide1,
    piece,
    outbox,
    in_sem,
    pre_sem,
    own_sem,
    send0,
    recv0,
    send1,
    recv1,
    send2,
    recv2,
    send3,
    recv3,
):
    links = Links()
    count, stored = tiles.shape[0], tiles.shape[1]
    blks = links.blks
    chunk = count // CHUNKS
    loads = []
    for k, (source, target) in enumerate(((rhs_h, rhs), (smo_h, smo), (tiles_h, tiles))):
        for part in range(CHUNKS):
            rows = pl.ds(part * chunk, chunk)
            loads.append(
                pltpu.make_async_copy(
                    source.at[rows], target.at[rows], in_sem.at[k, part]
                )
            )
    for part in range(CHUNKS):
        loads[part].start()
        loads[CHUNKS + part].start()
    for part in range(CHUNKS):
        loads[2 * CHUNKS + part].start()
    barrier = pltpu.get_barrier_semaphore()
    links.greet_blk(barrier)

    def goal_copy(k):
        return remote(
            goals.at[k],
            goals_o.at[k],
            send3.at[k],
            recv3.at[k],
            links.along_blk(k),
        )

    def piece_copy(k):
        return remote(
            outbox.at[k],
            recv_o.at[k],
            send2.at[k],
            recv2.at[k],
            links.along_blk(k),
        )

    own_goals = pltpu.make_async_copy(goals.at[0], goals_o.at[0], own_sem.at[0])
    own_piece = pltpu.make_async_copy(outbox.at[0], recv_o.at[0], own_sem.at[1])
    own_goals.start()

    halos0, halos1 = [], []
    for part in range(CHUNKS):
        loads[part].wait()
        loads[CHUNKS + part].wait()

        def first_rows(rows):
            fresh = [times(rhs[i].astype(BF16), smo[i]) for i in rows]
            for i, z in zip(rows, fresh):
                pre[i] = z
                wide0[count + i] = z.astype(BF16)

        for_rows(part * chunk, chunk, first_rows)
        if part == 0:
            pl.semaphore_wait(barrier, blks - 1)
        for copy in halo_copies(
            links, wide0, count, part * chunk, chunk, send0, recv0, part
        ):
            copy.start()
            halos0.append(copy)

    for part in range(CHUNKS):
        loads[2 * CHUNKS + part].wait()
    for copy in halos0:
        copy.wait_recv()

    for part in range(CHUNKS):

        def sweep_rows(rows):
            resid = [
                (rhs[i] - applied(tiles, cols, wide0, i, stored)).astype(BF16)
                for i in rows
            ]
            fresh = [pre[i] + times(g, smo[i]) for i, g in zip(rows, resid)]
            for i, z in zip(rows, fresh):
                pre[i] = z
                wide1[count + i] = z.astype(BF16)

        for_rows(part * chunk, chunk, sweep_rows)
        for copy in halo_copies(
            links, wide1, count, part * chunk, chunk, send1, recv1, part
        ):
            copy.start()
            halos1.append(copy)
    keep = pltpu.make_async_copy(pre, pre_o, pre_sem)
    keep.start()

    def goal_step(k, carry):
        goal_copy(k).start()
        return carry

    lax.fori_loop(1, blks, goal_step, 0)
    for copy in halos1:
        copy.wait_recv()

    def piece_rows(rows):
        resid = [
            (rhs[i] - applied(tiles, cols, wide1, i, stored)).astype(BF16)
            for i in rows
        ]
        sums = [times(g, chosen(slots, i)) for i, g in zip(rows, resid)]
        for i, z in zip(rows, sums):
            piece[i] = z.astype(BF16)

    for_rows(0, count, piece_rows)

    def pack(k):
        for s in range(CAP):
            outbox[k, s] = piece[sidx[k * CAP + s]]

    def send_step(k, carry):
        pack(k)
        piece_copy(k).start()
        return carry

    lax.fori_loop(1, blks, send_step, 0)
    pack(0)
    own_piece.start()
    for copy in halos0 + halos1:
        copy.wait_send()

    def end_step(k, carry):
        goal_copy(k).wait()
        piece_copy(k).wait()
        return carry

    lax.fori_loop(1, blks, end_step, 0)
    own_goals.wait()
    own_piece.wait()
    keep.wait()


def up_kernel(
    goals,
    mcols,
    ccols,
    low,
    places,
    fcols,
    recv_h,
    mtiles_h,
    msmo_h,
    mslots,
    ctiles_h,
    csmo_h,
    rhs_h,
    pre_h,
    tiles_h,
    smo_h,
    slots,
    fine_o,
    mid_o,
    coarse_o,
    inbox,
    mtiles,
    msmo,
    ctiles,
    csmo,
    rhs,
    pre,
    tiles,
    smo,
    mrhs,
    mpre,
    mpiece,
    mwide,
    mfield,
    mround,
    parts,
    fold_send,
    fold_recv,
    crhs,
    cfield,
    cwide,
    gathered,
    coarse,
    outbox,
    backbox,
    fwide,
    in_sem,
    out_sem,
    msend,
    mrecv,
    rsend,
    rrecv,
    csend,
    crecv,
    gsend,
    grecv,
    bsend,
    brecv,
    fsend,
    frecv,
):
    links = Links()
    folds, blks = links.folds, links.blks
    count, stored = tiles.shape[0], tiles.shape[1]
    mcount = mtiles.shape[0]
    half = ctiles.shape[0]
    wide_r = crhs.shape[1]
    groups = folds // 2
    core = lax.rem(links.fold, 2)
    group = links.fold // 2
    sources = (
        (recv_h, inbox),
        (msmo_h, msmo),
        (mtiles_h, mtiles),
        (csmo_h.at[pl.ds(core * half, half)], csmo),
        (ctiles_h.at[pl.ds(core * half, half)], ctiles),
        (rhs_h, rhs),
        (pre_h, pre),
        (tiles_h, tiles),
        (smo_h, smo),
    )
    loads = [
        pltpu.make_async_copy(source, target, in_sem.at[k])
        for k, (source, target) in enumerate(sources)
    ]
    for load in loads:
        load.start()
    barrier = pltpu.get_barrier_semaphore()
    links.greet_blk(barrier)
    links.greet_fold(barrier)

    loads[0].wait()
    zero = jnp.zeros(mrhs.shape[1:], F32)
    tied = group_of(mcount, 12)
    for first in range(0, mcount, tied):

        def add_piece(p, sums):
            src, s = p // CAP, lax.rem(p, CAP)
            value = inbox[src, s].astype(F32)
            goal = goals[src, 0, s]
            return tuple(
                total + jnp.where(goal == first + t, value, zero)
                for t, total in enumerate(sums)
            )

        sums = lax.fori_loop(0, blks * CAP, add_piece, (zero,) * tied)
        for t, total in enumerate(sums):
            mrhs[first + t] = total
    loads[1].wait()

    def mid_first(rows):
        fresh = [times(mrhs[i].astype(BF16), msmo[i]) for i in rows]
        for i, z in zip(rows, fresh):
            mpre[i] = z
            mwide[0][mcount + i] = z.astype(BF16)

    for_rows(0, mcount, mid_first)
    pl.semaphore_wait(barrier, blks - 1 + folds - 1)

    def mid_halo(k):
        return halo_copies(
            links, mwide[k], mcount, 0, mcount, msend.at[k], mrecv.at[k], 0
        )

    def start_halo(copies):
        for copy in copies:
            copy.start()

    def end_halo(copies):
        for copy in copies:
            copy.wait()

    start_halo(mid_halo(0))
    loads[2].wait()
    end_halo(mid_halo(0))

    def mid_sweep(rows):
        resid = [
            (mrhs[i] - applied(mtiles, mcols, mwide[0], i, stored)).astype(BF16)
            for i in rows
        ]
        fresh = [mpre[i] + times(g, msmo[i]) for i, g in zip(rows, resid)]
        for i, z in zip(rows, fresh):
            mpre[i] = z
            mwide[1][mcount + i] = z.astype(BF16)

    for_rows(0, mcount, mid_sweep)
    start_halo(mid_halo(1))
    end_halo(mid_halo(1))

    def mid_pieces(rows):
        resid = [
            (mrhs[i] - applied(mtiles, mcols, mwide[1], i, stored)).astype(BF16)
            for i in rows
        ]
        sums = [times(g, chosen(mslots, i)) for i, g in zip(rows, resid)]
        for i, z in zip(rows, sums):
            mpiece[i] = z

    for_rows(0, mcount, mid_pieces)

    def low_terms(c, carry):
        total = zero
        for j in range(mcount):
            total = total + jnp.where(low[j] == c, mpiece[j], zero)
        place = c // half
        row = lax.rem(c, half)
        for g in range(groups):
            parts[2 * g + place, row] = total[g * wide_r : (g + 1) * wide_r]
        return carry

    lax.fori_loop(0, 2 * half, low_terms, 0)
    fold_send[...] = parts[...].astype(BF16)

    def fold_copy(k):
        to = links.along_fold(k)
        return remote(
            fold_send.at[to[0]], fold_recv.at[k], rsend.at[k], rrecv.at[k], to
        )

    for k in range(1, folds):
        fold_copy(k).start()
    fold_recv[0] = fold_send[links.fold]
    loads[3].wait()
    loads[4].wait()
    for k in range(1, folds):
        fold_copy(k).wait()
    total = fold_recv[0].astype(F32)
    for k in range(1, folds):
        total = total + fold_recv[k].astype(F32)
    crhs[...] = total

    mine = 2 * half + core * half

    def coarse_copies(k):
        own = cwide[k].at[pl.ds(mine, half)]
        other = links.fold + 1 - 2 * core
        copies = []
        place = 0
        for step, offset in ((0, 1), (1, 0), (-1, 2)):
            blk = lax.rem(links.blk + step + blks, blks)
            for fold in (other,) if step == 0 else (links.fold, other):
                copies.append(
                    remote(
                        own,
                        cwide[k].at[pl.ds(offset * 2 * half + core * half, half)],
                        csend.at[k, place],
                        crecv.at[k, place],
                        (fold, blk),
                    )
                )
                place += 1
        return copies

    def coarse_first(rows):
        fresh = [times(crhs[i].astype(BF16), csmo[i]) for i in rows]
        for i, z in zip(rows, fresh):
            cfield[i] = z
            cwide[0][mine + i] = z.astype(BF16)

    for_rows(0, half, coarse_first)

    for k in range(COARSE - 1):
        start_halo(coarse_copies(k))
        end_halo(coarse_copies(k))

        def coarse_sweep(rows):
            resid = [
                (crhs[i] - applied(ctiles, ccols, cwide[k], i, stored)).astype(BF16)
                for i in rows
            ]
            fresh = [cfield[i] + times(g, csmo[i]) for i, g in zip(rows, resid)]
            for i, z in zip(rows, fresh):
                cfield[i] = z
                cwide[k + 1][mine + i] = z.astype(BF16)

        for_rows(0, half, coarse_sweep)

    def gather_copy(k):
        return remote(
            cwide[COARSE - 1].at[pl.ds(mine, half)],
            gathered.at[links.fold],
            gsend.at[k],
            grecv.at[k],
            links.along_fold(k),
        )

    for k in range(1, folds):
        gather_copy(k).start()
    gathered[links.fold] = cwide[COARSE - 1][pl.ds(mine, half)]
    for k in range(1, folds):
        gather_copy(k).wait()
    for f in range(folds):
        g, place = f // 2, f % 2
        coarse[pl.ds(place * half, half), pl.ds(g * wide_r, wide_r), :] = gathered[
            f
        ].astype(F32)
    keep_coarse = pltpu.make_async_copy(coarse, coarse_o, out_sem.at[0])
    keep_coarse.start()

    def mid_lift(rows):
        lifted = [
            jnp.dot(
                coarse[low[i]].astype(BF16),
                chosen(mslots, i),
                preferred_element_type=F32,
            )
            for i in rows
        ]
        fresh = [mpre[i] + z for i, z in zip(rows, lifted)]
        for i, z in zip(rows, fresh):
            mpre[i] = z
            mwide[2][mcount + i] = z.astype(BF16)

    for_rows(0, mcount, mid_lift)
    start_halo(mid_halo(2))
    end_halo(mid_halo(2))

    def mid_last(rows):
        resid = [
            (mrhs[i] - applied(mtiles, mcols, mwide[2], i, stored)).astype(BF16)
            for i in rows
        ]
        fresh = [mpre[i] + times(g, msmo[i]) for i, g in zip(rows, resid)]
        for i, z in zip(rows, fresh):
            mfield[i] = z
            mround[i] = z.astype(BF16)

    for_rows(0, mcount, mid_last)
    keep_mid = pltpu.make_async_copy(mfield, mid_o, out_sem.at[1])
    keep_mid.start()


    def back_copy(k):
        return remote(
            outbox.at[k],
            backbox.at[pl.ds(k * CAP, CAP)],
            bsend.at[k],
            brecv.at[k],
            links.along_blk(k),
        )

    def back_step(k, carry):
        back = lax.rem(blks - k, blks)
        for s in range(CAP):
            outbox[k, s] = mround[jnp.minimum(goals[back, 0, s], mcount - 1)]
        back_copy(k).start()
        return carry

    lax.fori_loop(1, blks, back_step, 0)
    for s in range(CAP):
        backbox[s] = mround[jnp.minimum(goals[0, 0, s], mcount - 1)]
    for k in (5, 6, 7, 8):
        loads[k].wait()

    def back_end(k, carry):
        back_copy(k).wait()
        return carry

    lax.fori_loop(1, blks, back_end, 0)

    chunk = count // CHUNKS
    halos = []
    for part in range(CHUNKS):

        def fine_lift(rows):
            lifted = [
                jnp.dot(
                    backbox[places[i]], chosen(slots, i), preferred_element_type=F32
                )
                for i in rows
            ]
            fresh = [pre[i] + z for i, z in zip(rows, lifted)]
            for i, z in zip(rows, fresh):
                pre[i] = z
                fwide[count + i] = z.astype(BF16)

        for_rows(part * chunk, chunk, fine_lift)
        for copy in halo_copies(
            links, fwide, count, part * chunk, chunk, fsend, frecv, part
        ):
            copy.start()
            halos.append(copy)
    for copy in halos:
        copy.wait()
    keeps = []
    for part in range(CHUNKS):

        def fine_last(rows):
            resid = [
                (rhs[i] - applied(tiles, fcols, fwide, i, stored)).astype(BF16)
                for i in rows
            ]
            fresh = [pre[i] + times(g, smo[i]) for i, g in zip(rows, resid)]
            for i, z in zip(rows, fresh):
                pre[i] = z

        for_rows(part * chunk, chunk, fine_last)
        rows = pl.ds(part * chunk, chunk)
        keeps.append(
            pltpu.make_async_copy(pre.at[rows], fine_o.at[rows], out_sem.at[2 + part])
        )
        keeps[-1].start()
    for copy in [keep_coarse, keep_mid] + keeps:
        copy.wait()


def local_columns(columns, per_device):
    blks = lax.axis_size("blk")
    owner = columns // per_device % blks
    offset = (owner - lax.axis_index("blk") + 1 + blks) % blks
    return (offset * per_device + columns % per_device).reshape(-1)


ANY = pl.BlockSpec(memory_space=pl.ANY)
SMEM = pl.BlockSpec(memory_space=pltpu.SMEM)
VMEM = pl.BlockSpec(memory_space=pltpu.VMEM)


def on_device(
    fine_rhs,
    fine_tiles,
    fine_cols,
    fine_smoother,
    fine_map,
    fine_slots,
    mid_tiles,
    mid_cols,
    mid_smoother,
    mid_map,
    mid_slots,
    coarse_tiles,
    coarse_cols,
    coarse_smoother,
):
    count, stored, width, _ = fine_tiles.shape
    mcount = mid_tiles.shape[0]
    lcount = coarse_tiles.shape[0]
    r = fine_rhs.shape[1]
    folds, blks = lax.axis_size("fold"), lax.axis_size("blk")
    half = lcount // 2
    wide_r = r * 2 // folds
    block = (r, width)

    owner = fine_map // mcount % blks
    steps = (owner - lax.axis_index("blk") + blks) % blks
    order = jnp.arange(count, dtype=jnp.int32)
    same = (steps[:, None] == steps[None, :]) & (order[None, :] < order[:, None])
    rank = jnp.sum(same.astype(jnp.int32), axis=1)
    position = steps * CAP + rank
    hit = position[None, :] == jnp.arange(blks * CAP, dtype=jnp.int32)[:, None]
    sidx = jnp.sum(jnp.where(hit, order[None, :], 0), axis=1)
    goal = jnp.sum(jnp.where(hit, (fine_map % mcount)[None, :] - mcount, 0), axis=1) + mcount
    goals = jnp.pad(goal.reshape(blks, 1, CAP), ((0, 0), (0, 0), (0, 128 - CAP)))
    places = (blks - steps) % blks * CAP + rank
    fcols = local_columns(fine_cols, count)

    dma = pltpu.SemaphoreType.DMA
    pre, received, goals_in = pl.pallas_call(
        down_kernel,
        out_shape=(
            jax.ShapeDtypeStruct((count,) + block, F32),
            jax.ShapeDtypeStruct((blks, CAP) + block, BF16),
            jax.ShapeDtypeStruct((blks, 1, 128), jnp.int32),
        ),
        in_specs=[SMEM, SMEM, ANY, ANY, ANY, VMEM, VMEM],
        out_specs=(ANY, ANY, ANY),
        scratch_shapes=[
            pltpu.VMEM((count,) + block, F32),
            pltpu.VMEM((count, stored, width, width), BF16),
            pltpu.VMEM((count, width, width), BF16),
            pltpu.VMEM((count,) + block, F32),
            pltpu.VMEM((3 * count,) + block, BF16),
            pltpu.VMEM((3 * count,) + block, BF16),
            pltpu.VMEM((count,) + block, BF16),
            pltpu.VMEM((blks, CAP) + block, BF16),
            dma((3, CHUNKS)),
            dma(()),
            dma((2,)),
        ]
        + [dma((2, CHUNKS))] * 4
        + [dma((blks,))] * 4,
        compiler_params=pltpu.CompilerParams(
            collective_id=1, has_side_effects=True, vmem_limit_bytes=40 << 20
        ),
        name="fine_down",
    )(fcols, sidx, fine_rhs, fine_tiles, fine_smoother, fine_slots, goals)

    fine, mid, coarse = pl.pallas_call(
        up_kernel,
        out_shape=(
            jax.ShapeDtypeStruct((count,) + block, F32),
            jax.ShapeDtypeStruct((mcount,) + block, F32),
            jax.ShapeDtypeStruct((lcount,) + block, F32),
        ),
        in_specs=[SMEM] * 6 + [ANY] * 3 + [VMEM] + [ANY] * 6 + [VMEM],
        out_specs=(ANY, ANY, ANY),
        scratch_shapes=[
            pltpu.VMEM((blks, CAP) + block, BF16),
            pltpu.VMEM((mcount, stored, width, width), BF16),
            pltpu.VMEM((mcount, width, width), BF16),
            pltpu.VMEM((half, stored, width, width), BF16),
            pltpu.VMEM((half, width, width), BF16),
            pltpu.VMEM((count,) + block, F32),
            pltpu.VMEM((count,) + block, F32),
            pltpu.VMEM((count, stored, width, width), BF16),
            pltpu.VMEM((count, width, width), BF16),
            pltpu.VMEM((mcount,) + block, F32),
            pltpu.VMEM((mcount,) + block, F32),
            pltpu.VMEM((mcount,) + block, F32),
            [pltpu.VMEM((3 * mcount,) + block, BF16)] * 3,
            pltpu.VMEM((mcount,) + block, F32),
            pltpu.VMEM((mcount,) + block, BF16),
            pltpu.VMEM((folds, half, wide_r, width), F32),
            pltpu.VMEM((folds, half, wide_r, width), BF16),
            pltpu.VMEM((folds, half, wide_r, width), BF16),
            pltpu.VMEM((half, wide_r, width), F32),
            pltpu.VMEM((half, wide_r, width), F32),
            [pltpu.VMEM((3 * lcount, wide_r, width), BF16)] * COARSE,
            pltpu.VMEM((folds, half, wide_r, width), BF16),
            pltpu.VMEM((lcount,) + block, F32),
            pltpu.VMEM((blks, CAP) + block, BF16),
            pltpu.VMEM((blks * CAP,) + block, BF16),
            pltpu.VMEM((3 * count,) + block, BF16),
            dma((9,)),
            dma((2 + CHUNKS,)),
            dma((3, 2, 1)),
            dma((3, 2, 1)),
            dma((folds,)),
            dma((folds,)),
            dma((COARSE - 1, 5)),
            dma((COARSE - 1, 5)),
            dma((folds,)),
            dma((folds,)),
            dma((blks,)),
            dma((blks,)),
            dma((2, CHUNKS)),
            dma((2, CHUNKS)),
        ],
        compiler_params=pltpu.CompilerParams(
            collective_id=2, has_side_effects=True, vmem_limit_bytes=48 << 20
        ),
        name="coarse_and_up",
    )(
        goals_in,
        local_columns(mid_cols, mcount),
        local_columns(coarse_cols, lcount)
        .reshape(2, half * stored)[lax.axis_index("fold") % 2],
        mid_map % lcount,
        places,
        fcols,
        received,
        mid_tiles,
        mid_smoother,
        mid_slots,
        coarse_tiles,
        coarse_smoother,
        fine_rhs,
        pre,
        fine_tiles,
        fine_smoother,
        fine_slots,
    )
    return fine, mid, coarse


def solution(mesh):
    both = ("fold", "blk")
    placed = (
        P(both, None, None),
        P(both, None, None, None),
        P(both, None),
        P(both, None, None),
        P(both),
        P(both, None),
        P(both, None, None, None),
        P(both, None),
        P(both, None, None),
        P(both),
        P(both, None),
        P("blk", None, None, None),
        P("blk", None),
        P("blk", None, None),
    )
    return jax.shard_map(
        on_device,
        mesh=mesh,
        in_specs=placed,
        out_specs=(P(both, None, None), P(both, None, None), P("blk", None, None)),
        check_vma=False,
    )
```

time: 622 us -> 197 us (0.32)
  waiting for transfers between devices: 458 us -> 0 us
  Pallas kernels: 0 us -> 180 us
  matrix products: 93 us -> 0 us
  starting transfers between devices: 32.1 us -> 0 us
  between operations: 14.1 us -> 0.75 us
    reduce_scatter x1 -> x0, waiting for transfers between devices: 217 us -> none  [on_device(): lax.psum_scatter(jnp.einsum('tj,jrs->trs', picking, pieces, precision=lax...]
    pallas_call x0 -> x2, Pallas kernels: none -> 180 us  [the longest x1 119 us: on_device(): pl.pallas_call(up_kernel, out_shape=(jax.ShapeDtypeStruct((count,) + bloc...]
    dot_general x37 -> x0, matrix products: 93 us -> none  [the longest x14 60.3 us: smooth_tiles(): jnp.einsum('iuw,irw->iru', smoother, resid.astype(jnp.bfloat16), preferre...]
    ppermute x26 -> x0, waiting for transfers between devices: 91.6 us -> none  [the longest x13 51.4 us: extended(): before = lax.ppermute(last, axis, up)]
    all_gather x1 -> x0, waiting for transfers between devices: 83.8 us -> none  [on_device(): lax.all_gather(mid_field.astype(jnp.bfloat16), 'blk', axis=0, tiled=True)]
    psum x1 -> x0, waiting for transfers between devices: 66.1 us -> none  [on_device(): lax.psum(low_terms.astype(jnp.bfloat16), 'fold').astype(jnp.float32)]
    ppermute x26 -> x0, starting transfers between devices: 32 us -> none  [the longest x13 19.2 us: extended(): after = lax.ppermute(first, axis, down)]
    unnamed x46 -> x19, local copies, waits for them, and re-layouts: 1.1 us -> 8.82 us
  transfers between devices with their start and end apart: 29 -> 0, of which waited for: 29 -> 0; matrix products, arithmetic and copies ran while one was open for 1% -> 0% of each run, Pallas kernels for 0% -> 0%
where the time goes in v1:
time: 197 us; the launch traced here: 194 us
  Pallas kernels  180 us (91%)
  local copies, waits for them, and re-layouts  9.51 us (5%)
  other arithmetic  3.8 us (2%)
    pallas_call x1, Pallas kernels, on_device(): pl.pallas_call(up_kernel, out_shape=(jax.ShapeDtypeStruct((count,) + bloc...  119 us
    pallas_call x1, Pallas kernels, on_device(): pl.pallas_call(down_kernel, out_shape=(jax.ShapeDtypeStruct((count,) + bl...  60.8 us
    unnamed x19, local copies, waits for them, and re-layouts  8.82 us

profile of v1, /device:TPU:1, one launch (start us, length us, event | category | flops | bytes accessed | tf_op | source)
XLA Modules:
  0.0 194.3 jit_solution(2230052893348845618)
XLA Ops:
  0.6 0.7 and_select_fusion.1.low
  1.3 0.7 and_select_fusion.3
  2.0 0.2 convert_reduce_fusion
  2.2 0.1 select_reduce_fusion
  2.3 0.7 fusion.6
  3.0 0.7 fusion.12
  3.7 0.7 fusion.18
  4.5 0.1 copy.26
  4.6 0.1 reshape.31.mcols
  4.6 0.1 copy.27
  4.7 0.1 reshape_reshape.3
  4.8 0.1 add.158
  5.0 0.1 copy.24
  5.0 0.1 reshape.30.cols.fcols
  5.2 0.0 copy-start
  5.2 3.2 %copy-done = bf16[48,5,128,128]{3,2,1,0:T(8,128)(2,1)S(1)} copy-done((bf16[48,5,128,128]{3,2,1,0:T(8,128)(2,1)S(1)}, bf16[48,5,128,128]{3,2,1,0:T(8,128)(2,1)}, u32[]{:S(2)}) %copy-start) | copy-done | bytes 7864344
  8.4 1.4 copy-done.1
  9.8 1.1 copy-done.2
  11.0 0.7 copy-done.6
  11.7 60.8 %fine_down.1 = (f32[48,32,128]{2,1,0:T(8,128)S(1)}, bf16[32,3,32,128]{3,2,1,0:T(8,128)(2,1)S(1)}, s32[32,1,128]{2,1,0:T(1,128)S(1)}) custom-call(s32[240]{0:T(256)S(1)} %reshape.30.cols.fcols, s32[96]{0:T(128)S(1)} %get-tuple-element.10.sidx, f32[48,32,128]{2,1,0:T(8,128)S(1)} %copy-done.2, bf16[48,5,128,128]{3,2,1,0:T(8,128)(2,1)S(1)} %copy-done, ...), custom_call_target="tpu_custom_call" | custom-call | tf_op jit(solution)/shard_map/fine_down/pallas_call | solution.py:700
  72.5 119.5 %coarse_and_up.1 = (f32[48,32,128]{2,1,0:T(8,128)S(1)}, f32[12,32,128]{2,1,0:T(8,128)S(1)}, f32[24,32,128]{2,1,0:T(8,128)S(1)}) custom-call(s32[32,1,128]{2,1,0:T(1,128)S(1)} %get-tuple-element.6.goals, s32[60]{0:T(128)S(1)} %reshape.31.mcols, s32[60]{0:T(128)S(1)} %dynamic-slice_bitcast_fusion.ccols, s32[12]{0:T(128)S(1)} %and_select_fusion.1.low, ...), custom_call_target="tpu_custom_call" | custom-call | tf_op jit(solution)/shard_map/coarse_and_up/pallas_call | solution.py:730
  192.0 0.9 copy.31
  192.9 0.7 copy.32
  193.6 0.7 copy.33
  (15 shorter events, 0.1 us)
Async XLA Ops:
  5.2 3.2 %copy-start = (bf16[48,5,128,128]{3,2,1,0:T(8,128)(2,1)S(1)}, bf16[48,5,128,128]{3,2,1,0:T(8,128)(2,1)}, u32[]{:S(2)}) copy-start(bf16[48,5,128,128]{3,2,1,0:T(8,128)(2,1)} %tiles_h.3) | copy-start | bytes 23592964
  8.4 1.4 copy-start.1
  9.8 1.1 copy-start.2
  10.9 0.7 copy-start.6
  11.7 60.8 %copy-start.3 = (f32[48,32,128]{2,1,0:T(8,128)S(1)}, f32[48,32,128]{2,1,0:T(8,128)}, u32[]{:S(2)}) copy-start(f32[48,32,128]{2,1,0:T(8,128)} %rhs_h.3) | copy-start | bytes 2359300
  11.7 60.8 %copy-start.4 = (bf16[24,128,128]{2,1,0:T(8,128)(2,1)S(1)}, bf16[24,128,128]{2,1,0:T(8,128)(2,1)}, u32[]{:S(2)}) copy-start(bf16[24,128,128]{2,1,0:T(8,128)(2,1)} %csmo_h.1) | copy-start | bytes 2359300
  11.7 60.8 %copy-start.5 = (bf16[12,128,128]{2,1,0:T(8,128)(2,1)S(1)}, bf16[12,128,128]{2,1,0:T(8,128)(2,1)}, u32[]{:S(2)}) copy-start(bf16[12,128,128]{2,1,0:T(8,128)(2,1)} %msmo_h.1) | copy-start | bytes 1179652
  11.7 60.8 %copy-start.7 = (s32[12,128]{1,0:T(8,128)S(1)}, s32[12,128]{1,0:T(8,128)}, u32[]{:S(2)}) copy-start(s32[12,128]{1,0:T(8,128)} %mslots.1) | copy-start | bytes 18436

commit v2 on v0

v2 whole, which is shorter than its diff:
```python
import jax
import jax.numpy as jnp
from jax import lax
from jax.experimental import pallas as pl
from jax.experimental.pallas import tpu as pltpu
from jax.sharding import PartitionSpec as P

COARSE = 8
CAP = 3
HALVES = 2
PARTS = 2
SPLIT = 2
SLOTS = 8
MESH = pl.DeviceIdType.MESH
F32 = jnp.float32
BF16 = jnp.bfloat16
I32 = jnp.int32


def times(left, right):
    return lax.dot_general(
        left, right, (((1,), (1,)), ((), ())), preferred_element_type=F32
    )


def group_of(count, most):
    return max(size for size in range(1, most + 1) if count % size == 0)


def for_rows(start, count, body, most=12):
    size = group_of(count, most)

    def step(turn, carry):
        first = start + turn * size
        body([first + k for k in range(size)])
        return carry

    lax.fori_loop(0, count // size, step, 0)


def each(first, last, body):
    def step(k, carry):
        body(k)
        return carry

    lax.fori_loop(first, last, step, 0)


def chosen(slots, row):
    line = slots[pl.ds(row, 1), :]
    width = line.shape[1]
    places = lax.broadcasted_iota(I32, (width, width), 0)
    return jnp.where(places == line, 1.0, 0.0).astype(BF16)


def remote(source, target, send, recv, device):
    return pltpu.make_async_remote_copy(
        src_ref=source,
        dst_ref=target,
        send_sem=send,
        recv_sem=recv,
        device_id=device,
        device_id_type=MESH,
    )


def within(index, size):
    return jnp.minimum(jnp.maximum(index, 0), size - 1)


class Level:
    def __init__(self, tiles, cols, first, span, start=0):
        self.tiles, self.cols, self.start = tiles, cols, start
        self.first, self.span = first, span

    def own(self, row, value):
        return times(value, self.tiles[row, 0])

    def others(self, row, wide):
        stored = self.tiles.shape[1]
        picked = []
        for k in range(1, stored):
            at = self.cols[k, self.start + row] - self.first
            at = jnp.where(at < 0, at + self.span, at)
            at = jnp.where(at >= self.span, at - self.span, at)
            picked.append(wide[within(at, wide.shape[0])])
        tile = jnp.concatenate([self.tiles[row, k] for k in range(1, stored)], axis=1)
        return times(jnp.concatenate(picked, axis=1), tile)


def cycle(
    fcols,
    mcols,
    ccols,
    low,
    fmap,
    slots,
    mslots,
    rhs_h,
    tiles_h,
    smo_h,
    mtiles_h,
    msmo_h,
    ctiles_h,
    csmo_h,
    fine_o,
    mid_o,
    coarse_o,
    v,
    w,
    q,
):
    fold, blk = lax.axis_index("fold"), lax.axis_index("blk")
    folds, blks = lax.axis_size("fold"), lax.axis_size("blk")
    tiles, smo, rhs, pre = v["tiles"], v["smo"], v["rhs"], v["pre"]
    mtiles, msmo, mrhs, mpre = v["mtiles"], v["msmo"], v["mrhs"], v["mpre"]
    ctiles, csmo, crhs, cfield = v["ctiles"], v["csmo"], v["crhs"], v["cfield"]
    count, mcount, half = tiles.shape[0], mtiles.shape[0], ctiles.shape[0]
    rh = rhs.shape[1] // HALVES
    chunk = count // PARTS
    wide_r = crhs.shape[1]
    groups = folds // 2
    core = lax.rem(fold, 2)
    sent = []

    def along_blk(step):
        return (fold, lax.rem(blk + step + blks, blks))

    def along_fold(step):
        return (lax.rem(fold + step, folds), blk)

    def load(source, target, place, start=0, rows=None):
        if rows is not None:
            source, target = source.at[pl.ds(start, rows)], target.at[pl.ds(start, rows)]
        return pltpu.make_async_copy(source, target, q["load"].at[place])

    first_loads = []
    for part in range(PARTS):
        first_loads.append(load(rhs_h, rhs, 2 * part, part * chunk, chunk))
        first_loads.append(load(smo_h, smo, 2 * part + 1, part * chunk, chunk))
    tile_load = load(tiles_h, tiles, 2 * PARTS)
    later = [
        load(msmo_h, msmo, 2 * PARTS + 1),
        load(mtiles_h, mtiles, 2 * PARTS + 2),
        load(csmo_h.at[pl.ds(core * half, half)], csmo, 2 * PARTS + 3),
        load(ctiles_h.at[pl.ds(core * half, half)], ctiles, 2 * PARTS + 4),
    ]
    for copy in first_loads + [tile_load]:
        copy.start()

    barrier = pltpu.get_barrier_semaphore()

    def greet(device):
        pl.semaphore_signal(barrier, inc=1, device_id=device, device_id_type=MESH)

    each(1, blks, lambda k: greet(along_blk(k)))
    each(1, folds, lambda k: greet(along_fold(k)))

    fine = Level(tiles, fcols, (fold * blks + blk - 1) * count, blks * count)
    mid = Level(mtiles, mcols, (fold * blks + blk - 1) * mcount, blks * mcount)
    low_level = Level(
        ctiles, ccols, (blk - 1) * 2 * half, blks * 2 * half, core * half
    )

    def halo(wide, size, start, rows, sems, place):
        own = wide.at[pl.ds(size + start, rows)]
        return [
            remote(
                own,
                wide.at[pl.ds(at + start, rows)],
                q[sems + "_send"].at[place, side],
                q[sems + "_recv"].at[place, side],
                along_blk(step),
            )
            for side, (at, step) in enumerate(((0, 1), (2 * size, -1)))
        ]

    def send(copies):
        for copy in copies:
            copy.start()
        sent.extend(copies)

    def received(copies):
        for copy in copies:
            copy.wait_recv()

    def fine_halo(turn, h, part):
        place = (turn * HALVES + h) * PARTS + part
        return halo(w["wide"][turn * HALVES + h], count, part * chunk, chunk, "halo", place)

    def fine_wide(turn, h):
        return w["wide"][turn * HALVES + h]

    def fine_received(turn, h):
        for part in range(PARTS):
            received(fine_halo(turn, h, part))

    def part_of_r(h):
        return pl.ds(h * rh, rh)

    for part in range(PARTS):
        first_loads[2 * part].wait()
        first_loads[2 * part + 1].wait()

        def first_rows(rows):
            fresh = [times(rhs[i].astype(BF16), smo[i]) for i in rows]
            for i, z in zip(rows, fresh):
                pre[i] = z
                for h in range(HALVES):
                    fine_wide(0, h)[count + i] = z[h * rh : (h + 1) * rh].astype(BF16)

        for_rows(part * chunk, chunk, first_rows)
        if part == 0:
            pl.semaphore_wait(barrier, blks - 1 + folds - 1)
        send(fine_halo(0, 0, part))
    for h in range(1, HALVES):
        for part in range(PARTS):
            send(fine_halo(0, h, part))
    for copy in later:
        copy.start()

    line = fmap[...] - fold * blks * mcount
    owner = lax.shift_right_logical(line * (-(-(1 << 19) // mcount)), 19)
    target = line - owner * mcount
    steps = owner - blk
    steps = jnp.where(steps < 0, steps + blks, steps)
    across = lax.broadcasted_iota(I32, (count, count), 1)
    down = lax.broadcasted_iota(I32, (count, count), 0)
    steps_down = jnp.sum(jnp.where(across == down, steps, 0), axis=1, keepdims=True)
    ahead = (steps_down == steps) & (down < across)
    rank = jnp.sum(jnp.where(ahead, 1, 0), axis=0, keepdims=True)
    position = steps * SLOTS + rank
    hit = lax.broadcasted_iota(I32, (blks * SLOTS, count), 0) == position
    order = lax.broadcasted_iota(I32, (blks * SLOTS, count), 1)
    index = jnp.sum(jnp.where(hit, order, 0), axis=1, keepdims=True)
    goal = jnp.sum(jnp.where(hit, target - mcount, 0), axis=1, keepdims=True) + mcount
    lane = lax.broadcasted_iota(I32, (blks * SLOTS, 128), 1)
    table = jnp.where(lane == 0, goal, index)
    v["table"][...] = table.reshape(blks, SLOTS, 128)
    back_steps = jnp.where(steps == 0, 0, blks - steps)
    v["places"][pl.ds(0, 1), pl.ds(0, count)] = back_steps * CAP + rank

    def small(source, target, place):
        return pltpu.make_async_copy(source, target, q["small"].at[place])

    own_table = small(v["table"], v["table_s"], 0)
    own_places = small(v["places"], v["places_s"], 1)
    own_table.start()
    own_places.start()

    def goal_copy(k):
        return remote(
            v["table"].at[k],
            v["goals"].at[k],
            q["goal_send"].at[k],
            q["goal_recv"].at[k],
            along_blk(k),
        )

    each(1, blks, lambda k: goal_copy(k).start())
    v["goals"][0] = v["table"][0]

    def fine_own(turn, h):
        def rows_of(rows):
            fresh = [
                rhs[i, part_of_r(h), :] - fine.own(i, fine_wide(turn, h)[count + i])
                for i in rows
            ]
            for i, z in zip(rows, fresh):
                w["base"][h][i] = z

        for_rows(0, count, rows_of)

    def fine_resid(turn, h, i):
        return (w["base"][h][i] - fine.others(i, fine_wide(turn, h))).astype(BF16)

    tile_load.wait()
    for h in range(HALVES):
        fine_own(0, h)

    for h in range(HALVES):
        fine_received(0, h)
        for part in range(PARTS):

            def sweep_rows(rows):
                resid = [fine_resid(0, h, i) for i in rows]
                fresh = [
                    pre[i, part_of_r(h), :] + times(g, smo[i])
                    for i, g in zip(rows, resid)
                ]
                for i, z in zip(rows, fresh):
                    pre[i, part_of_r(h), :] = z
                    fine_wide(1, h)[count + i] = z.astype(BF16)

            for_rows(part * chunk, chunk, sweep_rows)
            send(fine_halo(1, h, part))
    for h in range(HALVES):
        fine_own(1, h)
    own_table.wait()
    own_places.wait()

    def piece_copy(h, k):
        return remote(
            w["outbox"][h].at[k],
            w["inbox"][h].at[k],
            q["piece_send"].at[h, k],
            q["piece_recv"].at[h, k],
            along_blk(k),
        )

    for h in range(HALVES):
        fine_received(1, h)
        piece = w["piece"][h]

        def piece_rows(rows):
            resid = [fine_resid(1, h, i) for i in rows]
            sums = [times(g, chosen(slots, i)) for i, g in zip(rows, resid)]
            for i, z in zip(rows, sums):
                piece[i] = z.astype(BF16)

        for_rows(0, count, piece_rows)

        def pack(k):
            for s in range(CAP):
                w["outbox"][h][k, s] = piece[within(v["table_s"][k, s, 1], count)]
            piece_copy(h, k).start()

        each(1, blks, pack)
        for s in range(CAP):
            w["inbox"][h][0, s] = piece[within(v["table_s"][0, s, 1], count)]

    each(1, blks, lambda k: goal_copy(k).wait_recv())
    goals_move = small(v["goals"], v["goals_s"], 2)
    goals_move.start()
    goals_move.wait()
    goals = v["goals_s"]

    zero = jnp.zeros((rh, rhs.shape[2]), F32)
    tied = group_of(mcount, 12)
    for h in range(HALVES):
        each(1, blks, lambda k: piece_copy(h, k).wait_recv())
        for first in range(0, mcount, tied):

            def add_pieces(k, sums):
                for s in range(CAP):
                    value = w["inbox"][h][k, s].astype(F32)
                    place = goals[k, s, 0]
                    sums = tuple(
                        total + jnp.where(place == first + t, value, zero)
                        for t, total in enumerate(sums)
                    )
                return sums

            sums = lax.fori_loop(0, blks, add_pieces, (zero,) * tied)
            for t, total in enumerate(sums):
                mrhs[first + t, part_of_r(h), :] = total
    for copy in later[:2]:
        copy.wait()

    def mid_put(turn, rows, fresh):
        for i, z in zip(rows, fresh):
            mpre[i] = z
            w["mwide"][turn][mcount + i] = z.astype(BF16)

    def mid_first(rows):
        mid_put(0, rows, [times(mrhs[i].astype(BF16), msmo[i]) for i in rows])

    def mid_exchange(turn):
        wide = w["mwide"][turn]
        copies = halo(wide, mcount, 0, mcount, "mid", turn)
        send(copies)

        def own_rows(rows):
            fresh = [mrhs[i] - mid.own(i, wide[mcount + i]) for i in rows]
            for i, z in zip(rows, fresh):
                v["mbase"][i] = z

        for_rows(0, mcount, own_rows)
        received(copies)

    def mid_resid(turn, i):
        return (v["mbase"][i] - mid.others(i, w["mwide"][turn])).astype(BF16)

    for_rows(0, mcount, mid_first)
    mid_exchange(0)

    def mid_sweep(rows):
        resid = [mid_resid(0, i) for i in rows]
        mid_put(1, rows, [mpre[i] + times(g, msmo[i]) for i, g in zip(rows, resid)])

    for_rows(0, mcount, mid_sweep)
    mid_exchange(1)

    def mid_pieces(rows):
        resid = [mid_resid(1, i) for i in rows]
        sums = [times(g, chosen(mslots, i)) for i, g in zip(rows, resid)]
        for i, z in zip(rows, sums):
            v["mpiece"][i] = z

    for_rows(0, mcount, mid_pieces)

    whole_zero = jnp.zeros(mrhs.shape[1:], F32)
    low_first = blk * 2 * half

    def low_terms(c):
        total = whole_zero
        for j in range(mcount):
            total = total + jnp.where(low[j] - low_first == c, v["mpiece"][j], whole_zero)
        place = c // half
        row = lax.rem(c, half)
        for g in range(groups):
            v["fold_out"][2 * g + place, row] = total[
                g * wide_r : (g + 1) * wide_r
            ].astype(BF16)

    each(0, 2 * half, low_terms)

    fold_copies = [
        remote(
            v["fold_out"].at[along_fold(k)[0]],
            v["fold_in"].at[k],
            q["fold_send"].at[k],
            q["fold_recv"].at[k],
            along_fold(k),
        )
        for k in range(1, folds)
    ]
    send(fold_copies)
    v["fold_in"][0] = v["fold_out"][fold]
    for copy in later[2:]:
        copy.wait()
    received(fold_copies)
    total = v["fold_in"][0].astype(F32)
    for k in range(1, folds):
        total = total + v["fold_in"][k].astype(F32)
    crhs[...] = total

    mine = 2 * half + core * half
    other = fold + 1 - 2 * core
    piece_rows_c = half // group_of(half, SPLIT)

    def coarse_copies(turn):
        wide = w["cwide"][turn]
        copies = []
        place = 0
        for step, offset in ((1, 0), (-1, 2), (0, 1)):
            for device in (other,) if step == 0 else (fold, other):
                for part in range(half // piece_rows_c):
                    rows = part * piece_rows_c
                    copies.append(
                        remote(
                            wide.at[pl.ds(mine + rows, piece_rows_c)],
                            wide.at[
                                pl.ds(
                                    offset * 2 * half + core * half + rows, piece_rows_c
                                )
                            ],
                            q["coarse_send"].at[turn, place],
                            q["coarse_recv"].at[turn, place],
                            (device, lax.rem(blk + step + blks, blks)),
                        )
                    )
                    place += 1
        return copies

    def coarse_put(turn, rows, fresh):
        for i, z in zip(rows, fresh):
            cfield[i] = z
            w["cwide"][turn][mine + i] = z.astype(BF16)

    def coarse_first(rows):
        coarse_put(0, rows, [times(crhs[i].astype(BF16), csmo[i]) for i in rows])

    for_rows(0, half, coarse_first)
    for turn in range(COARSE - 1):
        wide = w["cwide"][turn]
        copies = coarse_copies(turn)
        send(copies)

        def coarse_own(rows):
            fresh = [crhs[i] - low_level.own(i, wide[mine + i]) for i in rows]
            for i, z in zip(rows, fresh):
                v["cbase"][i] = z

        for_rows(0, half, coarse_own)
        received(copies)

        def coarse_sweep(rows):
            resid = [
                (v["cbase"][i] - low_level.others(i, wide)).astype(BF16) for i in rows
            ]
            fresh = [cfield[i] + times(g, csmo[i]) for i, g in zip(rows, resid)]
            coarse_put(turn + 1, rows, fresh)

        for_rows(0, half, coarse_sweep)

    last_own = w["cwide"][COARSE - 1]
    gather_copies = [
        remote(
            last_own.at[pl.ds(mine, half)],
            v["gathered"].at[fold],
            q["gather_send"].at[k],
            q["gather_recv"].at[k],
            along_fold(k),
        )
        for k in range(1, folds)
    ]
    send(gather_copies)
    v["gathered"][fold] = last_own[pl.ds(mine, half)]
    received(gather_copies)
    for f in range(folds):
        g, place = f // 2, f % 2
        v["coarse"][pl.ds(place * half, half), pl.ds(g * wide_r, wide_r), :] = v[
            "gathered"
        ][f].astype(F32)
    keeps = [pltpu.make_async_copy(v["coarse"], coarse_o, q["keep"].at[0])]
    keeps[-1].start()

    def mid_lift(rows):
        lifted = [
            jnp.dot(
                v["coarse"][within(low[i] - low_first, 2 * half)].astype(BF16),
                chosen(mslots, i),
                preferred_element_type=F32,
            )
            for i in rows
        ]
        mid_put(2, rows, [mpre[i] + z for i, z in zip(rows, lifted)])

    for_rows(0, mcount, mid_lift)
    mid_exchange(2)

    def mid_last(rows):
        resid = [mid_resid(2, i) for i in rows]
        fresh = [mpre[i] + times(g, msmo[i]) for i, g in zip(rows, resid)]
        for i, z in zip(rows, fresh):
            v["mfield"][i] = z
            for h in range(HALVES):
                w["mround"][h][i] = z[h * rh : (h + 1) * rh].astype(BF16)

    for_rows(0, mcount, mid_last)

    def back_copy(h, k):
        return remote(
            w["backout"][h].at[k],
            w["backbox"][h].at[pl.ds(k * CAP, CAP)],
            q["back_send"].at[h, k],
            q["back_recv"].at[h, k],
            along_blk(k),
        )

    for h in range(HALVES):

        def wanted(k, s):
            place = goals[lax.rem(blks - k, blks), s, 0]
            return w["mround"][h][within(place, mcount)]

        def pack_back(k):
            for s in range(CAP):
                w["backout"][h][k, s] = wanted(k, s)
            back_copy(h, k).start()

        each(1, blks, pack_back)
        for s in range(CAP):
            w["backbox"][h][s] = wanted(0, s)
    keeps.append(pltpu.make_async_copy(v["mfield"], mid_o, q["keep"].at[1]))
    keeps[-1].start()

    for h in range(HALVES):
        each(1, blks, lambda k: back_copy(h, k).wait_recv())
        for part in range(PARTS):

            def fine_lift(rows):
                lifted = [
                    jnp.dot(
                        w["backbox"][h][within(v["places_s"][0, i], blks * CAP)],
                        chosen(slots, i),
                        preferred_element_type=F32,
                    )
                    for i in rows
                ]
                fresh = [pre[i, part_of_r(h), :] + z for i, z in zip(rows, lifted)]
                for i, z in zip(rows, fresh):
                    pre[i, part_of_r(h), :] = z
                    fine_wide(2, h)[count + i] = z.astype(BF16)

            for_rows(part * chunk, chunk, fine_lift)
            send(fine_halo(2, h, part))
    for h in range(HALVES):
        fine_own(2, h)
    for h in range(HALVES):
        fine_received(2, h)
        for part in range(PARTS):

            def fine_last(rows):
                resid = [fine_resid(2, h, i) for i in rows]
                fresh = [
                    pre[i, part_of_r(h), :] + times(g, smo[i])
                    for i, g in zip(rows, resid)
                ]
                for i, z in zip(rows, fresh):
                    pre[i, part_of_r(h), :] = z

            for_rows(part * chunk, chunk, fine_last)
            if h == HALVES - 1:
                rows = pl.ds(part * chunk, chunk)
                keeps.append(
                    pltpu.make_async_copy(
                        pre.at[rows], fine_o.at[rows], q["keep"].at[2 + part]
                    )
                )
                keeps[-1].start()

    for copy in sent:
        copy.wait_send()

    def end_sends(k):
        goal_copy(k).wait_send()
        for h in range(HALVES):
            piece_copy(h, k).wait_send()
            back_copy(h, k).wait_send()

    each(1, blks, end_sends)
    for copy in keeps:
        copy.wait()


def on_device(
    fine_rhs,
    fine_tiles,
    fine_cols,
    fine_smoother,
    fine_map,
    fine_slots,
    mid_tiles,
    mid_cols,
    mid_smoother,
    mid_map,
    mid_slots,
    coarse_tiles,
    coarse_cols,
    coarse_smoother,
):
    count, stored, width, _ = fine_tiles.shape
    mcount = mid_tiles.shape[0]
    lcount = coarse_tiles.shape[0]
    r = fine_rhs.shape[1]
    folds, blks = lax.axis_size("fold"), lax.axis_size("blk")
    half = lcount // 2
    rh, wide_r = r // HALVES, r * 2 // folds

    dma = pltpu.SemaphoreType.DMA

    def field(blocks, rows=r, kind=F32):
        return pltpu.VMEM((blocks, rows, width), kind)

    def tile(blocks, *more):
        return pltpu.VMEM((blocks, *more, width, width), BF16)

    arrays = {
        "tiles": tile(count, stored),
        "smo": tile(count),
        "rhs": field(count),
        "pre": field(count),
        "mtiles": tile(mcount, stored),
        "msmo": tile(mcount),
        "mrhs": field(mcount),
        "mpre": field(mcount),
        "mbase": field(mcount),
        "mpiece": field(mcount),
        "mfield": field(mcount),
        "ctiles": tile(half, stored),
        "csmo": tile(half),
        "crhs": field(half, wide_r),
        "cfield": field(half, wide_r),
        "cbase": field(half, wide_r),
        "fold_out": pltpu.VMEM((folds, half, wide_r, width), BF16),
        "fold_in": pltpu.VMEM((folds, half, wide_r, width), BF16),
        "gathered": pltpu.VMEM((folds, half, wide_r, width), BF16),
        "coarse": field(lcount),
        "table": pltpu.VMEM((blks, SLOTS, 128), I32),
        "goals": pltpu.VMEM((blks, SLOTS, 128), I32),
        "places": pltpu.VMEM((SLOTS, 128), I32),
        "table_s": pltpu.SMEM((blks, SLOTS, 128), I32),
        "goals_s": pltpu.SMEM((blks, SLOTS, 128), I32),
        "places_s": pltpu.SMEM((SLOTS, 128), I32),
    }
    box = pltpu.VMEM((blks, CAP, rh, width), BF16)
    several = {
        "wide": [field(3 * count, rh, BF16)] * (3 * HALVES),
        "base": [field(count, rh)] * HALVES,
        "piece": [field(count, rh, BF16)] * HALVES,
        "outbox": [box] * HALVES,
        "inbox": [box] * HALVES,
        "backout": [box] * HALVES,
        "backbox": [field(blks * CAP, rh, BF16)] * HALVES,
        "mwide": [field(3 * mcount, r, BF16)] * 3,
        "mround": [field(mcount, rh, BF16)] * HALVES,
        "cwide": [field(3 * lcount, wide_r, BF16)] * COARSE,
    }
    sems = {
        "load": dma((2 * PARTS + 5,)),
        "small": dma((3,)),
        "keep": dma((2 + PARTS,)),
    }
    for name, shape in (
        ("halo", (3 * HALVES * PARTS, 2)),
        ("mid", (3, 2)),
        ("goal", (blks,)),
        ("piece", (HALVES, blks)),
        ("back", (HALVES, blks)),
        ("fold", (folds,)),
        ("gather", (folds,)),
        ("coarse", (COARSE - 1, 5 * SPLIT)),
    ):
        sems[name + "_send"] = dma(shape)
        sems[name + "_recv"] = dma(shape)

    smem = pl.BlockSpec(memory_space=pltpu.SMEM)
    vmem = pl.BlockSpec(memory_space=pltpu.VMEM)
    hbm = pl.BlockSpec(memory_space=pltpu.HBM)
    return pl.pallas_call(
        cycle,
        out_shape=(
            jax.ShapeDtypeStruct((count, r, width), F32),
            jax.ShapeDtypeStruct((mcount, r, width), F32),
            jax.ShapeDtypeStruct((lcount, r, width), F32),
        ),
        in_specs=[smem] * 4 + [vmem] * 3 + [hbm] * 7,
        out_specs=(hbm, hbm, hbm),
        scratch_shapes=[arrays, several, sems],
        compiler_params=pltpu.CompilerParams(
            collective_id=1, has_side_effects=True, vmem_limit_bytes=56 << 20
        ),
        name="cycle",
    )(
        fine_cols.T,
        mid_cols.T,
        coarse_cols.T,
        mid_map,
        fine_map.reshape(1, count),
        fine_slots,
        mid_slots,
        fine_rhs,
        fine_tiles,
        fine_smoother,
        mid_tiles,
        mid_smoother,
        coarse_tiles,
        coarse_smoother,
    )


def solution(mesh):
    both = ("fold", "blk")
    placed = (
        P(both, None, None),
        P(both, None, None, None),
        P(both, None),
        P(both, None, None),
        P(both),
        P(both, None),
        P(both, None, None, None),
        P(both, None),
        P(both, None, None),
        P(both),
        P(both, None),
        P("blk", None, None, None),
        P("blk", None),
        P("blk", None, None),
    )
    return jax.shard_map(
        on_device,
        mesh=mesh,
        in_specs=placed,
        out_specs=(P(both, None, None), P(both, None, None), P("blk", None, None)),
        check_vma=False,
    )
```

time: 622 us -> 162 us (0.26)
  waiting for transfers between devices: 458 us -> 0 us
  Pallas kernels: 0 us -> 155 us
  matrix products: 93 us -> 0 us
  starting transfers between devices: 32.1 us -> 0 us
  between operations: 14.1 us -> 0.65 us
  other arithmetic: 8.65 us -> 0 us
    reduce_scatter x1 -> x0, waiting for transfers between devices: 217 us -> none  [on_device(): lax.psum_scatter(jnp.einsum('tj,jrs->trs', picking, pieces, precision=lax...]
    pallas_call x0 -> x1, Pallas kernels: none -> 155 us  [on_device(): pl.pallas_call(cycle, out_shape=(jax.ShapeDtypeStruct((count, r, width),...]
    dot_general x37 -> x0, matrix products: 93 us -> none  [the longest x14 60.3 us: smooth_tiles(): jnp.einsum('iuw,irw->iru', smoother, resid.astype(jnp.bfloat16), preferre...]
    ppermute x26 -> x0, waiting for transfers between devices: 91.6 us -> none  [the longest x13 51.4 us: extended(): before = lax.ppermute(last, axis, up)]
    all_gather x1 -> x0, waiting for transfers between devices: 83.8 us -> none  [on_device(): lax.all_gather(mid_field.astype(jnp.bfloat16), 'blk', axis=0, tiled=True)]
    psum x1 -> x0, waiting for transfers between devices: 66.1 us -> none  [on_device(): lax.psum(low_terms.astype(jnp.bfloat16), 'fold').astype(jnp.float32)]
    ppermute x26 -> x0, starting transfers between devices: 32 us -> none  [the longest x13 19.2 us: extended(): after = lax.ppermute(first, axis, down)]
    dot_general x1 -> x0, local copies, waits for them, and re-layouts: 6.32 us -> none  [on_device(): jnp.einsum('tj,jrs->trs', picking, pieces, precision=lax.Precision.HIGHEST)]
  transfers between devices with their start and end apart: 29 -> 0, of which waited for: 29 -> 0; matrix products, arithmetic and copies ran while one was open for 1% -> 0% of each run, Pallas kernels for 0% -> 0%
where the time goes in v2:
time: 162 us; the launch traced here: 161 us
  Pallas kernels  155 us (96%)
  local copies, waits for them, and re-layouts  5.44 us (3%)
    pallas_call x1, Pallas kernels, on_device(): pl.pallas_call(cycle, out_shape=(jax.ShapeDtypeStruct((count, r, width),...  155 us
    unnamed x3, local copies, waits for them, and re-layouts  5.44 us

profile of v2, /device:TPU:1, one launch (start us, length us, event | category | flops | bytes accessed | tf_op | source)
XLA Modules:
  0.0 161.4 jit_solution(1301598674263993668)
XLA Ops:
  0.6 155.3 %cycle.1 = (f32[48,32,128]{2,1,0:T(8,128)}, f32[12,32,128]{2,1,0:T(8,128)}, f32[24,32,128]{2,1,0:T(8,128)}) custom-call(s32[5,48]{1,0:T(8,128)} %bitcast.4, s32[5,12]{1,0:T(8,128)} %bitcast.5, s32[5,24]{1,0:T(8,128)} %bitcast.6, s32[12]{0:T(128)} %low.1, s32[1,48]{1,0:T(1,128)} %bitcast.7, s32[48,128]{1,0:T(8,128)} %slots.1, s32[12,128]{1,0:T(8,128)} %mslots.1, ...), custom_call_target="tpu_custom_call" | custom-call | tf_op jit(solution)/shard_map/cycle/pallas_call | solution.py:722
  155.9 2.1 %copy.20 = f32[48,32,128]{2,1,0:T(8,128)} copy(f32[48,32,128]{2,1,0:T(8,128)} %get-tuple-element.6) | data formatting | bytes 1572864
  158.0 1.6 %copy.21 = f32[12,32,128]{2,1,0:T(8,128)} copy(f32[12,32,128]{2,1,0:T(8,128)} %get-tuple-element.7) | data formatting | bytes 393216
  159.6 1.8 %copy.22 = f32[24,32,128]{2,1,0:T(8,128)} copy(f32[24,32,128]{2,1,0:T(8,128)} %get-tuple-element.8) | data formatting | bytes 786432

commit v3 on v2

--- a/solution.py
+++ b/solution.py
@@ -153,8 +153,27 @@
     def greet(device):
         pl.semaphore_signal(barrier, inc=1, device_id=device, device_id_type=MESH)
 
-    each(1, blks, lambda k: greet(along_blk(k)))
-    each(1, folds, lambda k: greet(along_fold(k)))
+    for step in (1, -1):
+        greet(along_blk(step))
+        greet(along_fold(step + folds))
+
+    def spread(along, size, first):
+        stages, reach = [], 1
+        while 2 * reach < size:
+            stages.append((along, reach, size, first + len(stages)))
+            reach *= 2
+        return stages
+
+    def spread_stage(stage):
+        along, reach, size, place = stage
+        for step in (reach, size - reach):
+            pl.semaphore_signal(
+                q["news"].at[place], inc=1, device_id=along(step), device_id_type=MESH
+            )
+        pl.semaphore_wait(q["news"].at[place], 2)
+
+    blk_news = spread(along_blk, blks, 0)
+    fold_news = spread(along_fold, folds, len(blk_news))
 
     fine = Level(tiles, fcols, (fold * blks + blk - 1) * count, blks * count)
     mid = Level(mtiles, mcols, (fold * blks + blk - 1) * mcount, blks * mcount)
@@ -211,7 +230,7 @@
 
         for_rows(part * chunk, chunk, first_rows)
         if part == 0:
-            pl.semaphore_wait(barrier, blks - 1 + folds - 1)
+            pl.semaphore_wait(barrier, 4)
         send(fine_halo(0, 0, part))
     for h in range(1, HALVES):
         for part in range(PARTS):
@@ -257,7 +276,6 @@
             along_blk(k),
         )
 
-    each(1, blks, lambda k: goal_copy(k).start())
     v["goals"][0] = v["table"][0]
 
     def fine_own(turn, h):
@@ -275,8 +293,13 @@
         return (w["base"][h][i] - fine.others(i, fine_wide(turn, h))).astype(BF16)
 
     tile_load.wait()
+    for stage in blk_news[:2]:
+        spread_stage(stage)
     for h in range(HALVES):
         fine_own(0, h)
+    for stage in blk_news[2:]:
+        spread_stage(stage)
+    each(1, blks, lambda k: goal_copy(k).start())
 
     for h in range(HALVES):
         fine_received(0, h)
@@ -296,6 +319,8 @@
             send(fine_halo(1, h, part))
     for h in range(HALVES):
         fine_own(1, h)
+    for stage in fold_news:
+        spread_stage(stage)
     own_table.wait()
     own_places.wait()
 
@@ -338,10 +363,11 @@
     zero = jnp.zeros((rh, rhs.shape[2]), F32)
     tied = group_of(mcount, 12)
     for h in range(HALVES):
-        each(1, blks, lambda k: piece_copy(h, k).wait_recv())
         for first in range(0, mcount, tied):
 
-            def add_pieces(k, sums):
+            def add_pieces(k, sums, wait=True):
+                if wait and first == 0:
+                    piece_copy(h, k).wait_recv()
                 for s in range(CAP):
                     value = w["inbox"][h][k, s].astype(F32)
                     place = goals[k, s, 0]
@@ -351,7 +377,8 @@
                     )
                 return sums
 
-            sums = lax.fori_loop(0, blks, add_pieces, (zero,) * tied)
+            sums = add_pieces(0, (zero,) * tied, wait=False)
+            sums = lax.fori_loop(1, blks, add_pieces, sums)
             for t, total in enumerate(sums):
                 mrhs[first + t, part_of_r(h), :] = total
     for copy in later[:2]:
@@ -702,6 +729,7 @@
         "load": dma((2 * PARTS + 5,)),
         "small": dma((3,)),
         "keep": dma((2 + PARTS,)),
+        "news": pltpu.SemaphoreType.REGULAR((8,)),
     }
     for name, shape in (
         ("halo", (3 * HALVES * PARTS, 2)),
@@ -719,6 +747,7 @@
     smem = pl.BlockSpec(memory_space=pltpu.SMEM)
     vmem = pl.BlockSpec(memory_space=pltpu.VMEM)
     hbm = pl.BlockSpec(memory_space=pltpu.HBM)
+    anywhere = pl.BlockSpec(memory_space=pl.ANY)
     return pl.pallas_call(
         cycle,
         out_shape=(
@@ -727,10 +756,10 @@
             jax.ShapeDtypeStruct((lcount, r, width), F32),
         ),
         in_specs=[smem] * 4 + [vmem] * 3 + [hbm] * 7,
-        out_specs=(hbm, hbm, hbm),
+        out_specs=(anywhere, anywhere, anywhere),
         scratch_shapes=[arrays, several, sems],
         compiler_params=pltpu.CompilerParams(
-            collective_id=1, has_side_effects=True, vmem_limit_bytes=56 << 20
+            collective_id=1, has_side_effects=True, vmem_limit_bytes=44 << 20
         ),
         name="cycle",
     )(

time: 162 us -> 174 us (1.074)
  local copies, waits for them, and re-layouts: 5.44 us -> 13.3 us
  Pallas kernels: 155 us -> 160 us
    unnamed x3 -> x27, local copies, waits for them, and re-layouts: 5.44 us -> 13.3 us
    pallas_call x1, Pallas kernels: 155 us -> 160 us  [on_device(): pl.pallas_call(cycle, out_shape=(jax.ShapeDtypeStruct((count, r, width),...]
where the time goes in v3:
time: 174 us; the launch traced here: 173 us
  Pallas kernels  160 us (92%)
  local copies, waits for them, and re-layouts  13.3 us (8%)
    pallas_call x1, Pallas kernels, on_device(): pl.pallas_call(cycle, out_shape=(jax.ShapeDtypeStruct((count, r, width),...  160 us
    unnamed x27, local copies, waits for them, and re-layouts  13.3 us

profile of v3, /device:TPU:1, one launch (start us, length us, event | category | flops | bytes accessed | tf_op | source)
XLA Modules:
  0.0 173.5 jit_solution(3462721864695247473)
XLA Ops:
  0.6 0.0 copy-start
  0.6 1.5 copy-done
  2.2 0.0 copy-start.1
  2.2 1.4 copy-done.1
  3.6 0.0 copy-start.2
  3.6 1.1 copy-done.2
  4.7 0.0 copy-start.3
  4.7 1.1 copy-done.3
  5.9 0.0 copy-start.4
  5.9 1.0 copy-done.4
  6.9 0.0 copy-start.5
  6.9 0.7 copy-done.5
  7.6 0.0 copy-start.6
  7.6 0.7 copy-done.6
  8.3 0.0 copy-start.7
  8.3 0.7 copy-done.7
  9.0 0.7 copy-done.8
  9.7 0.7 copy-done.9
  10.4 0.7 copy-done.10
  11.0 0.7 copy-done.11
  11.7 159.5 %cycle.1 = (f32[48,32,128]{2,1,0:T(8,128)S(1)}, f32[12,32,128]{2,1,0:T(8,128)S(1)}, f32[24,32,128]{2,1,0:T(8,128)S(1)}) custom-call(s32[5,48]{1,0:T(8,128)S(1)} %bitcast.4, s32[5,12]{1,0:T(8,128)S(1)} %bitcast.5, s32[5,24]{1,0:T(8,128)S(1)} %bitcast.6, s32[12]{0:T(128)S(1)} %copy-done.10, s32[1,48]{1,0:T(1,128)S(1)} %bitcast.7, s32[48,128]{1,0:T(8,128)S(1)} %copy-done.5, ...), custom_call_target="tpu_custom_call" | custom-call | tf_op jit(solution)/shard_map/cycle/pallas_call | solution.py:751
  171.2 0.9 copy.20
  172.1 0.7 copy.21
  172.7 0.7 copy.22
  (4 shorter events, 0.0 us)
Async XLA Ops:
  0.6 1.5 copy-start
  2.2 1.4 copy-start.1
  3.6 1.1 copy-start.2
  4.7 1.1 copy-start.3
  5.9 1.0 copy-start.4
  6.9 0.7 copy-start.5
  7.6 0.7 copy-start.6
  8.3 0.7 copy-start.7
  9.0 0.7 copy-start.8
  9.7 0.7 copy-start.9
  10.4 0.7 copy-start.10
  11.0 0.7 copy-start.11

commit v4 on v3

--- a/solution.py
+++ b/solution.py
@@ -89,13 +89,13 @@
 
 
 def cycle(
-    fcols,
-    mcols,
-    ccols,
-    low,
-    fmap,
-    slots,
-    mslots,
+    fcols_h,
+    mcols_h,
+    ccols_h,
+    low_h,
+    fmap_h,
+    slots_h,
+    mslots_h,
     rhs_h,
     tiles_h,
     smo_h,
@@ -145,7 +145,23 @@
         load(csmo_h.at[pl.ds(core * half, half)], csmo, 2 * PARTS + 3),
         load(ctiles_h.at[pl.ds(core * half, half)], ctiles, 2 * PARTS + 4),
     ]
-    for copy in first_loads + [tile_load]:
+    fcols, mcols, ccols, low = v["fcols"], v["mcols"], v["ccols"], v["low"]
+    fmap, slots, mslots = v["fmap"], v["slots"], v["mslots"]
+    table_loads = [
+        load(source, target, 2 * PARTS + 5 + k)
+        for k, (source, target) in enumerate(
+            (
+                (fmap_h, fmap),
+                (fcols_h, fcols),
+                (slots_h, slots),
+                (mcols_h, mcols),
+                (mslots_h, mslots),
+                (low_h, low),
+                (ccols_h, ccols),
+            )
+        )
+    ]
+    for copy in first_loads + table_loads[:3] + [tile_load]:
         copy.start()
 
     barrier = pltpu.get_barrier_semaphore()
@@ -164,16 +180,27 @@
             reach *= 2
         return stages
 
-    def spread_stage(stage):
-        along, reach, size, place = stage
-        for step in (reach, size - reach):
-            pl.semaphore_signal(
-                q["news"].at[place], inc=1, device_id=along(step), device_id_type=MESH
-            )
-        pl.semaphore_wait(q["news"].at[place], 2)
-
     blk_news = spread(along_blk, blks, 0)
     fold_news = spread(along_fold, folds, len(blk_news))
+    turns = []
+    for k in range(max(len(blk_news), len(fold_news)) + 1):
+        turns.append([news[k : k + 1] for news in (blk_news, fold_news)])
+    pending = []
+
+    def next_stage():
+        for place in pending:
+            pl.semaphore_wait(q["news"].at[place], 2)
+        pending.clear()
+        if turns:
+            for along, reach, size, place in sum(turns.pop(0), []):
+                for step in (reach, size - reach):
+                    pl.semaphore_signal(
+                        q["news"].at[place],
+                        inc=1,
+                        device_id=along(step),
+                        device_id_type=MESH,
+                    )
+                pending.append(place)
 
     fine = Level(tiles, fcols, (fold * blks + blk - 1) * count, blks * count)
     mid = Level(mtiles, mcols, (fold * blks + blk - 1) * mcount, blks * mcount)
@@ -235,8 +262,11 @@
     for h in range(1, HALVES):
         for part in range(PARTS):
             send(fine_halo(0, h, part))
-    for copy in later:
+    next_stage()
+    for copy in later + table_loads[3:]:
         copy.start()
+    for copy in table_loads[:3]:
+        copy.wait()
 
     line = fmap[...] - fold * blks * mcount
     owner = lax.shift_right_logical(line * (-(-(1 << 19) // mcount)), 19)
@@ -293,13 +323,10 @@
         return (w["base"][h][i] - fine.others(i, fine_wide(turn, h))).astype(BF16)
 
     tile_load.wait()
-    for stage in blk_news[:2]:
-        spread_stage(stage)
+    next_stage()
     for h in range(HALVES):
         fine_own(0, h)
-    for stage in blk_news[2:]:
-        spread_stage(stage)
-    each(1, blks, lambda k: goal_copy(k).start())
+        next_stage()
 
     for h in range(HALVES):
         fine_received(0, h)
@@ -317,10 +344,12 @@
 
             for_rows(part * chunk, chunk, sweep_rows)
             send(fine_halo(1, h, part))
+        next_stage()
+    while turns or pending:
+        next_stage()
+    each(1, blks, lambda k: goal_copy(k).start())
     for h in range(HALVES):
         fine_own(1, h)
-    for stage in fold_news:
-        spread_stage(stage)
     own_table.wait()
     own_places.wait()
 
@@ -363,11 +392,10 @@
     zero = jnp.zeros((rh, rhs.shape[2]), F32)
     tied = group_of(mcount, 12)
     for h in range(HALVES):
+        each(1, blks, lambda k: piece_copy(h, k).wait_recv())
         for first in range(0, mcount, tied):
 
-            def add_pieces(k, sums, wait=True):
-                if wait and first == 0:
-                    piece_copy(h, k).wait_recv()
+            def add_pieces(k, sums):
                 for s in range(CAP):
                     value = w["inbox"][h][k, s].astype(F32)
                     place = goals[k, s, 0]
@@ -377,11 +405,10 @@
                     )
                 return sums
 
-            sums = add_pieces(0, (zero,) * tied, wait=False)
-            sums = lax.fori_loop(1, blks, add_pieces, sums)
+            sums = lax.fori_loop(0, blks, add_pieces, (zero,) * tied)
             for t, total in enumerate(sums):
                 mrhs[first + t, part_of_r(h), :] = total
-    for copy in later[:2]:
+    for copy in later[:2] + table_loads[3:]:
         copy.wait()
 
     def mid_put(turn, rows, fresh):
@@ -705,6 +732,13 @@
         "fold_in": pltpu.VMEM((folds, half, wide_r, width), BF16),
         "gathered": pltpu.VMEM((folds, half, wide_r, width), BF16),
         "coarse": field(lcount),
+        "fcols": pltpu.SMEM((stored, count), I32),
+        "mcols": pltpu.SMEM((stored, mcount), I32),
+        "ccols": pltpu.SMEM((stored, lcount), I32),
+        "low": pltpu.SMEM((mcount,), I32),
+        "fmap": pltpu.VMEM((1, count), I32),
+        "slots": pltpu.VMEM((count, width), I32),
+        "mslots": pltpu.VMEM((mcount, width), I32),
         "table": pltpu.VMEM((blks, SLOTS, 128), I32),
         "goals": pltpu.VMEM((blks, SLOTS, 128), I32),
         "places": pltpu.VMEM((SLOTS, 128), I32),
@@ -726,7 +760,7 @@
         "cwide": [field(3 * lcount, wide_r, BF16)] * COARSE,
     }
     sems = {
-        "load": dma((2 * PARTS + 5,)),
+        "load": dma((2 * PARTS + 12,)),
         "small": dma((3,)),
         "keep": dma((2 + PARTS,)),
         "news": pltpu.SemaphoreType.REGULAR((8,)),
@@ -744,8 +778,6 @@
         sems[name + "_send"] = dma(shape)
         sems[name + "_recv"] = dma(shape)
 
-    smem = pl.BlockSpec(memory_space=pltpu.SMEM)
-    vmem = pl.BlockSpec(memory_space=pltpu.VMEM)
     hbm = pl.BlockSpec(memory_space=pltpu.HBM)
     anywhere = pl.BlockSpec(memory_space=pl.ANY)
     return pl.pallas_call(
@@ -755,7 +787,7 @@
             jax.ShapeDtypeStruct((mcount, r, width), F32),
             jax.ShapeDtypeStruct((lcount, r, width), F32),
         ),
-        in_specs=[smem] * 4 + [vmem] * 3 + [hbm] * 7,
+        in_specs=[hbm] * 14,
         out_specs=(anywhere, anywhere, anywhere),
         scratch_shapes=[arrays, several, sems],
         compiler_params=pltpu.CompilerParams(

time: 174 us -> 168 us (0.966)
  Pallas kernels: 160 us -> 153 us
    pallas_call x1, Pallas kernels: 160 us -> 153 us  [on_device(): pl.pallas_call(cycle, out_shape=(jax.ShapeDtypeStruct((count, r, width),...]
where the time goes in v4:
time: 168 us; the launch traced here: 167 us
  Pallas kernels  153 us (91%)
  local copies, waits for them, and re-layouts  13.3 us (8%)
    pallas_call x1, Pallas kernels, on_device(): pl.pallas_call(cycle, out_shape=(jax.ShapeDtypeStruct((count, r, width),...  153 us
    unnamed x27, local copies, waits for them, and re-layouts  13.3 us

profile of v4, /device:TPU:1, one launch (start us, length us, event | category | flops | bytes accessed | tf_op | source)
XLA Modules:
  0.0 167.4 jit_solution(6122641013590884117)
XLA Ops:
  0.6 0.0 copy-start
  0.6 1.5 copy-done
  2.2 0.0 copy-start.1
  2.2 1.4 copy-done.1
  3.6 0.0 copy-start.2
  3.6 1.1 copy-done.2
  4.7 0.0 copy-start.3
  4.7 1.1 copy-done.3
  5.9 0.0 copy-start.4
  5.9 1.0 copy-done.4
  6.9 0.0 copy-start.5
  6.9 0.7 copy-done.5
  7.6 0.0 copy-start.6
  7.6 0.7 copy-done.6
  8.3 0.0 copy-start.7
  8.3 0.7 copy-done.7
  9.0 0.7 copy-done.8
  9.7 0.7 copy-done.9
  10.4 0.7 copy-done.10
  11.0 0.7 copy-done.11
  11.7 153.4 %cycle.1 = (f32[48,32,128]{2,1,0:T(8,128)S(1)}, f32[12,32,128]{2,1,0:T(8,128)S(1)}, f32[24,32,128]{2,1,0:T(8,128)S(1)}) custom-call(s32[5,48]{1,0:T(8,128)S(1)} %bitcast.4, s32[5,12]{1,0:T(8,128)S(1)} %bitcast.5, s32[5,24]{1,0:T(8,128)S(1)} %bitcast.6, s32[12]{0:T(128)S(1)} %copy-done.10, s32[1,48]{1,0:T(1,128)S(1)} %bitcast.7, s32[48,128]{1,0:T(8,128)S(1)} %copy-done.5, ...), custom_call_target="tpu_custom_call" | custom-call | tf_op jit(solution)/shard_map/cycle/pallas_call | solution.py:783
  165.1 0.9 copy.20
  166.0 0.7 copy.21
  166.7 0.7 copy.22
  (4 shorter events, 0.0 us)
Async XLA Ops:
  0.6 1.5 copy-start
  2.2 1.4 copy-start.1
  3.6 1.1 copy-start.2
  4.7 1.1 copy-start.3
  5.9 1.0 copy-start.4
  6.9 0.7 copy-start.5
  7.6 0.7 copy-start.6
  8.3 0.7 copy-start.7
  9.0 0.7 copy-start.8
  9.7 0.7 copy-start.9
  10.4 0.7 copy-start.10
  11.0 0.7 copy-start.11

commit v5 on v4

--- a/solution.py
+++ b/solution.py
@@ -795,20 +795,25 @@
         ),
         name="cycle",
     )(
-        fine_cols.T,
-        mid_cols.T,
-        coarse_cols.T,
-        mid_map,
-        fine_map.reshape(1, count),
-        fine_slots,
-        mid_slots,
-        fine_rhs,
-        fine_tiles,
-        fine_smoother,
-        mid_tiles,
-        mid_smoother,
-        coarse_tiles,
-        coarse_smoother,
+        *(
+            pltpu.with_memory_space_constraint(value, pltpu.HBM)
+            for value in (
+                fine_cols.T,
+                mid_cols.T,
+                coarse_cols.T,
+                mid_map,
+                fine_map.reshape(1, count),
+                fine_slots,
+                mid_slots,
+                fine_rhs,
+                fine_tiles,
+                fine_smoother,
+                mid_tiles,
+                mid_smoother,
+                coarse_tiles,
+                coarse_smoother,
+            )
+        )
     )
 
 

time: 168 us -> 155 us (0.923)
  local copies, waits for them, and re-layouts: 13.3 us -> 2.3 us
    unnamed x27 -> x3, local copies, waits for them, and re-layouts: 13.3 us -> 2.3 us
where the time goes in v5:
time: 155 us
  Pallas kernels  152 us (98%)
  local copies, waits for them, and re-layouts  2.3 us (1%)
    pallas_call x1, Pallas kernels, on_device(): pl.pallas_call(cycle, out_shape=(jax.ShapeDtypeStruct((count, r, width),...  152 us

profile of v5, /device:TPU:1, one launch (start us, length us, event | category | flops | bytes accessed | tf_op | source)
XLA Modules:
  0.0 155.1 jit_solution(16304384463091758518)
XLA Ops:
  0.6 152.2 %cycle.1 = (f32[48,32,128]{2,1,0:T(8,128)S(1)}, f32[12,32,128]{2,1,0:T(8,128)S(1)}, f32[24,32,128]{2,1,0:T(8,128)S(1)}) custom-call(s32[5,48]{1,0:T(8,128)} %bitcast.4, s32[5,12]{1,0:T(8,128)} %bitcast.5, s32[5,24]{1,0:T(8,128)} %bitcast.6, s32[12]{0:T(128)} %low_h.1, s32[1,48]{1,0:T(1,128)} %bitcast.7, s32[48,128]{1,0:T(8,128)} %slots_h.1, ...), custom_call_target="tpu_custom_call" | custom-call | tf_op jit(solution)/shard_map/cycle/pallas_call | solution.py:783
  152.8 0.9 copy.20
  153.7 0.7 copy.21
  154.4 0.7 copy.22

commit v6 on v5

--- a/solution.py
+++ b/solution.py
@@ -27,7 +27,7 @@
     return max(size for size in range(1, most + 1) if count % size == 0)
 
 
-def for_rows(start, count, body, most=12):
+def for_rows(start, count, body, most=24):
     size = group_of(count, most)
 
     def step(turn, carry):
@@ -347,9 +347,7 @@
         next_stage()
     while turns or pending:
         next_stage()
-    each(1, blks, lambda k: goal_copy(k).start())
-    for h in range(HALVES):
-        fine_own(1, h)
+    fine_own(1, 0)
     own_table.wait()
     own_places.wait()
 
@@ -382,6 +380,10 @@
         each(1, blks, pack)
         for s in range(CAP):
             w["inbox"][h][0, s] = piece[within(v["table_s"][0, s, 1], count)]
+        if h == 0:
+            each(1, blks, lambda k: goal_copy(k).start())
+        if h + 1 < HALVES:
+            fine_own(1, h + 1)
 
     each(1, blks, lambda k: goal_copy(k).wait_recv())
     goals_move = small(v["goals"], v["goals_s"], 2)

time: 155 us -> 155 us (level)
  no operation moved by 1% of the time
where the time goes in v6:
time: 155 us
  Pallas kernels  152 us (98%)
  local copies, waits for them, and re-layouts  2.3 us (1%)
    pallas_call x1, Pallas kernels, on_device(): pl.pallas_call(cycle, out_shape=(jax.ShapeDtypeStruct((count, r, width),...  152 us

profile of v6, /device:TPU:1, one launch (start us, length us, event | category | flops | bytes accessed | tf_op | source)
XLA Modules:
  0.0 155.3 jit_solution(15751687550162638313)
XLA Ops:
  0.6 152.4 %cycle.1 = (f32[48,32,128]{2,1,0:T(8,128)S(1)}, f32[12,32,128]{2,1,0:T(8,128)S(1)}, f32[24,32,128]{2,1,0:T(8,128)S(1)}) custom-call(s32[5,48]{1,0:T(8,128)} %bitcast.4, s32[5,12]{1,0:T(8,128)} %bitcast.5, s32[5,24]{1,0:T(8,128)} %bitcast.6, s32[12]{0:T(128)} %low_h.1, s32[1,48]{1,0:T(1,128)} %bitcast.7, s32[48,128]{1,0:T(8,128)} %slots_h.1, ...), custom_call_target="tpu_custom_call" | custom-call | tf_op jit(solution)/shard_map/cycle/pallas_call | solution.py:785
  153.0 0.9 copy.20
  153.9 0.7 copy.21
  154.6 0.7 copy.22
